TPU v7x, 32 devices: a whole 2x2x4 slice. The times are simulated.
32 devices in a mesh: groups: 2 (over x), dap: 16 (over z, y, core).
Axes of the slice: x: 2, y: 2, z: 4, core: 2. Of those that a mesh axis runs over, the one named last changes fastest.
Arguments:
- homolog_tensor: bfloat16 [128, 32, 256], P(('groups', 'dap')), parts along dimension 0, may hold values from -1 to 1
- couple_tensor: bfloat16 [64, 32, 128], P(('groups', 'dap')), parts along dimension 0, may hold values from -6 to 6
- horizontal_drop_filter: int32 [64, 256], P('groups'), parts along dimension 0, may hold values 0 or 1
- couple_offset_matrix: bfloat16 [128, 8], replicated, may hold values from -0.29882812 to 0.29882812
- horizontal_attend_matrix: bfloat16 [256, 1024], replicated, may hold values from -0.375 to 0.375
- horizontal_exit_matrix: bfloat16 [256, 256], replicated, may hold values from -0.375 to 0.375
- vertical_attend_matrix: bfloat16 [256, 1024], replicated, may hold values from -0.375 to 0.375
- vertical_exit_matrix: bfloat16 [256, 256], replicated, may hold values from -0.375 to 0.375
- averaged_product_flanks: bfloat16 [256, 64], replicated, may hold values from -0.375 to 0.375
- averaged_product_exit: bfloat16 [1024, 128], replicated, may hold values from -1 to 1
Outputs:
- alignment_output: bfloat16 [128, 32, 256], P('groups', 'dap'), parts along dimension 0
- pair_output_state: bfloat16 [64, 32, 128], P(('groups', 'dap')), parts along dimension 0
There are 2 independent parts, one for each index of `groups`. A program takes and returns all parts, laid end to end along the dimension named above; an argument that names none is the same for every part. Nothing has to cross between parts.
All inputs are finite; a program needn't handle non-finite values.
Results may differ from a plain program's by a relative error of at most 0.012.
Values may be sent and summed in bfloat16 or wider, within the bound.
No kernel may reach another device: no remote copies, remote signals or barrier semaphores. Data moves between devices by JAX's collectives and lax.ppermute only.
A program may use at most 64 MiB of HBM per device.

v0:
```python
import jax
import jax.numpy as jnp
from jax import lax
from jax.sharding import PartitionSpec as P

HEAD_NUMBER = 8
HEAD_WIDTH = 32
FACTOR_FEATURES = 32


def standardise_features(values):
    values = values.astype(jnp.float32)
    center = values - jnp.mean(values, axis=-1, keepdims=True)
    spread = jnp.mean(center * center, axis=-1, keepdims=True)
    return center * lax.rsqrt(spread + 1e-05)


def attend(normed, w_qkvg, w_out, bias):
    batch, length = (normed.shape[0], normed.shape[1])
    proj = jnp.einsum("blc,cf->blf", normed, w_qkvg, preferred_element_type=jnp.float32)
    proj = proj.reshape(batch, length, 4, HEAD_NUMBER, HEAD_WIDTH)
    query = (proj[:, :, 0] * HEAD_WIDTH ** (-0.5)).astype(jnp.bfloat16)
    keys = proj[:, :, 1].astype(jnp.bfloat16)
    values = proj[:, :, 2].astype(jnp.bfloat16)
    gate = proj[:, :, 3]
    if bias is None:
        bias = jnp.zeros((HEAD_NUMBER, length, length), jnp.bfloat16)

    def one_head(items):
        qh, kh, vh, bh = items
        scores = jnp.einsum("bid,bjd->bij", qh, kh, preferred_element_type=jnp.float32)
        scores = scores + bh.astype(jnp.float32)[None]
        weights = jax.nn.softmax(scores, axis=-1).astype(jnp.bfloat16)
        return jnp.einsum("bij,bjd->bid", weights, vh, preferred_element_type=jnp.float32)

    heads = lax.map(
        one_head,
        (jnp.moveaxis(query, 2, 0), jnp.moveaxis(keys, 2, 0), jnp.moveaxis(values, 2, 0), bias),
    )
    heads = jnp.moveaxis(heads, 0, 2)
    gated = (
        (jax.nn.sigmoid(gate) * heads)
        .astype(jnp.bfloat16)
        .reshape(batch, length, HEAD_NUMBER * HEAD_WIDTH)
    )
    return jnp.einsum("blk,kc->blc", gated, w_out, preferred_element_type=jnp.float32)


def shards(
    homolog_tensor,
    couple_tensor,
    horizontal_drop_filter,
    couple_offset_matrix,
    horizontal_attend_matrix,
    horizontal_exit_matrix,
    vertical_attend_matrix,
    vertical_exit_matrix,
    averaged_product_flanks,
    averaged_product_exit,
):
    normed_pair = standardise_features(couple_tensor).astype(jnp.bfloat16)
    own_bias = jnp.einsum(
        "ijz,zh->hij", normed_pair, couple_offset_matrix, preferred_element_type=jnp.float32
    ).astype(jnp.bfloat16)
    bias = lax.all_gather(own_bias, "dap", axis=1, tiled=True)
    starting_answer = standardise_features(homolog_tensor).astype(jnp.bfloat16)
    perform_refresh = attend(
        starting_answer, horizontal_attend_matrix, horizontal_exit_matrix, bias
    )
    homolog_later = (
        homolog_tensor.astype(jnp.float32)
        + horizontal_drop_filter.astype(jnp.float32) * (1.0 / 0.9) * perform_refresh
    ).astype(jnp.bfloat16)
    incoming_blocks = lax.all_to_all(homolog_later, "dap", split_axis=1, concat_axis=0, tiled=True)
    column_layout = jnp.swapaxes(incoming_blocks, 0, 1)
    perform_refresh = attend(
        standardise_features(column_layout).astype(jnp.bfloat16),
        vertical_attend_matrix,
        vertical_exit_matrix,
        None,
    )
    alignment_output = jnp.swapaxes(
        (column_layout.astype(jnp.float32) + perform_refresh).astype(jnp.bfloat16), 0, 1
    )
    final_result = standardise_features(alignment_output).astype(jnp.bfloat16)
    factors = jnp.einsum(
        "sic,cf->sif", final_result, averaged_product_flanks, preferred_element_type=jnp.float32
    )
    left = factors[..., :FACTOR_FEATURES].astype(jnp.bfloat16)
    right = factors[..., FACTOR_FEATURES:].astype(jnp.bfloat16)
    total = left.shape[0]
    own_rows = left.shape[1]
    whole = lax.all_gather(right, "dap", axis=1, tiled=True)
    outer = jnp.einsum("sic,sjd->ijcd", left, whole, preferred_element_type=jnp.float32) / total
    outer = outer.astype(jnp.bfloat16).reshape(
        own_rows, whole.shape[1], FACTOR_FEATURES * FACTOR_FEATURES
    )
    change = jnp.einsum(
        "ijk,kz->ijz", outer, averaged_product_exit, preferred_element_type=jnp.float32
    )
    pair_output_state = (couple_tensor.astype(jnp.float32) + change).astype(jnp.bfloat16)
    return (alignment_output, pair_output_state)


def solution(mesh):
    placed = (
        P(("groups", "dap"), None, None),
        P(("groups", "dap"), None, None),
        P("groups", None),
        P(),
        P(),
        P(),
        P(),
        P(),
        P(),
        P(),
    )
    return jax.shard_map(
        shards,
        mesh=mesh,
        in_specs=placed,
        out_specs=(P("groups", "dap", None), P(("groups", "dap"), None, None)),
        check_vma=False,
    )
```

profile of v0, /device:TPU:0, one launch (start us, length us, event | category | flops | bytes accessed | tf_op | source)
XLA Modules:
  0.0 80.2 jit_solution(14656866743398978957)
XLA Ops:
  0.6 1.0 %convert_reduce_fusion = f32[4,32]{1,0:T(4,128)S(1)} fusion(bf16[4,32,256]{2,1,0:T(8,128)(2,1)} %param.14), kind=kLoop, calls=%fused_computation.81 | loop fusion | flops 65408 | bytes 66048 | tf_op jit(solution)/shard_map/reduce_sum | solution.py:13
  1.7 1.0 %fusion.104 = f32[4,32]{1,0:T(4,128)S(1)} fusion(bf16[4,32,256]{2,1,0:T(8,128)(2,1)} %param.14, f32[4,32]{1,0:T(4,128)S(1)} %broadcast_multiply_fusion), kind=kLoop, calls=%fused_computation.88 | loop fusion | flops 130944 | bytes 66560 | tf_op jit(solution)/shard_map/reduce_sum | solution.py:14
  2.7 1.1 %fusion.87 = f32[4,32,1024]{2,1,0:T(8,128)S(1)} fusion(bf16[256,1024]{1,0:T(8,128)(2,1)S(1)} %copy-done, bf16[4,32,256]{2,1,0:T(8,128)(2,1)} %param.14, f32[4,32]{1,0:T(4,128)S(1)} %add_rsqrt_fusion, f32[4,32]{1,0:T(4,128)S(1)} %broadcast_multiply_fusion), kind=kOutput, calls=%fused_computation.63 | convolution fusion | flops 67239936 | bytes 1115136 | tf_op jit(solution)/shard_map/blc,cf->blf/dot_general | solution.py:20
  3.8 0.7 reshape.102
  4.5 2.6 %copy.41 = f32[4,32,4,8,32]{4,1,0,3,2:T(8,128)} copy(f32[4,32,4,8,32]{4,3,2,1,0:T(8,128)S(1)} %reshape.102) | data formatting | bytes 1048576 | tf_op jit(solution)/shard_map/reshape | solution.py:21
  7.1 2.2 %copy.76 = bf16[4,32,4,8,32]{4,1,0,3,2:T(8,128)(2,1)} copy(f32[4,32,4,8,32]{4,3,2,1,0:T(8,128)S(1)} %reshape.102) | data formatting | bytes 786432 | tf_op jit(solution)/shard_map/reshape | solution.py:21
  9.3 1.1 %fusion.90 = bf16[8,4,32,32]{3,2,1,0:T(8,128)(2,1)S(1)} fusion(f32[4,32,4,8,32]{4,1,0,3,2:T(8,128)} %copy.41), kind=kLoop, calls=%fused_computation.66 | loop fusion | flops 65536 | bytes 196608 | tf_op jit(solution)/shard_map/transpose | solution.py:38
  10.4 1.1 %slice_bitcast_fusion = (bf16[8,4,32,32]{3,2,1,0:T(8,128)(2,1)S(1)}, bf16[8,4,32,32]{3,2,1,0:T(8,128)(2,1)S(1)}) fusion(bf16[4,32,4,8,32]{4,1,0,3,2:T(8,128)(2,1)} %copy.76), kind=kLoop, calls=%fused_computation.75 | loop fusion | bytes 262144 | tf_op jit(solution)/shard_map/transpose | solution.py:38
  11.6 0.2 fusion.121
  11.7 0.2 fusion.78
  11.9 23.3 %all_gather.6 = bf16[8,32,32]{2,0,1:T(8,128)(2,1)S(1)} all-gather(bf16[8,2,32]{2,0,1:T(8,128)(2,1)S(1)} %fusion.78), channel_id=1, replica_groups=mesh['groups'=2,'dap'=16] {'dap'}, dimensions={1}, use_global_device_ids=true | all-gather | bytes 17408 | tf_op jit(solution)/shard_map/all_gather | solution.py:65
  35.2 0.1 copy.44
  35.4 4.3 %while.20 = (s32[]{:T(128)}, f32[8,4,32,32]{3,2,1,0:T(8,128)S(1)}, bf16[8,4,32,32]{3,2,1,0:T(8,128)(2,1)S(1)}, bf16[8,4,32,32]{3,2,1,0:T(8,128)(2,1)S(1)}, bf16[...) while((s32[]{:T(128)}, f32[8,4,32,32]{3,2,1,0:T(8,128)S(1)}, ...), condition=%wide.region_7.8_spmd, body=%wide.region_4.7_spmd.sunk | while | flops 816320 | bytes 274001 | solution.py:36
  35.4 0.2 fusion.161
  35.6 0.3 fusion.162
  36.0 0.2 fusion.161
  36.1 0.3 fusion.162
  36.5 0.2 fusion.161
  36.7 0.3 fusion.162
  37.0 0.2 fusion.161
  37.2 0.3 fusion.162
  37.6 0.2 fusion.161
  37.7 0.3 fusion.162
  38.1 0.2 fusion.161
  38.3 0.3 fusion.162
  38.6 0.2 fusion.161
  38.8 0.3 fusion.162
  39.1 0.2 fusion.161
  39.3 0.3 fusion.162
  39.7 1.3 %fusion.89 = bf16[4,32,8,32]{3,1,0,2:T(8,128)(2,1)S(1)} fusion(f32[8,4,32,32]{3,2,1,0:T(8,128)S(1)} %get-tuple-element.61, f32[4,32,4,8,32]{4,1,0,3,2:T(8,128)} %copy.41), kind=kLoop, calls=%fused_computation.65 | loop fusion | flops 163840 | bytes 327680 | tf_op jit(solution)/shard_map/convert_element_type | solution.py:43
  40.9 0.2 copy.45
  41.1 0.2 reshape.103
  41.3 0.2 fusion.76
  41.5 0.7 copy.46
  42.2 3.5 %all-to-all-start = ((bf16[4,32,256]{2,0,1:T(4,128)(2,1)}), bf16[4,32,256]{2,0,1:T(4,128)(2,1)S(1)}, u32[]{:S(2)}, u32[]{:S(2)}) async-start(bf16[4,32,256]{2,0,1:T(4,128)(2,1)} %copy.46), calls=%async_computation | async-start | bytes 131072 | tf_op jit(solution)/shard_map/all_to_all | solution.py:74
  45.7 6.8 %all-to-all-done = bf16[4,32,256]{2,0,1:T(4,128)(2,1)S(1)} async-done(((bf16[4,32,256]{2,0,1:T(4,128)(2,1)}), bf16[4,32,256]{2,0,1:T(4,128)(2,1)S(1)}, u32[]{:S(2)}, u32[]{:S(2)}) %all-to-all-start) | async-done | bytes 65568 | tf_op jit(solution)/shard_map/all_to_all | solution.py:74
  52.7 0.2 multiply_reduce_fusion
  52.9 0.4 fusion.85
  53.5 4.7 %while.21 = (s32[]{:T(128)}, f32[8,2,64,32]{2,3,0,1:T(8,128)S(1)}, bf16[8,2,64,32]{2,3,0,1:T(8,128)(2,1)S(1)}, bf16[8,2,64,32]{2,3,0,1:T(8,128)(2,1)S(1)}, bf16[8,2,64,32]{2,3,0,1:T(8,128)(2,1)S(1)}, /*index=5*/s32[]{:T(128)}) while((s32[]{:T(128)}, f32[8,2,64,32]{2,3,0,1:T(8,128)S(1)}, bf16[8,2,64,32]{2,3,0,1:T(8,128)(2,1)S(1)}, ...), condition=%wide.region_13.14_spmd, body=%wide.region_10.13_spmd.sunk | while | flops 1614080 | bytes 119365 | solution.py:36
  53.5 0.2 fusion.168
  53.8 0.3 fusion.169
  54.1 0.2 fusion.168
  54.4 0.3 fusion.169
  54.7 0.2 fusion.168
  55.0 0.3 fusion.169
  55.3 0.2 fusion.168
  55.6 0.3 fusion.169
  55.9 0.2 fusion.168
  56.1 0.3 fusion.169
  56.5 0.2 fusion.168
  56.7 0.3 fusion.169
  57.1 0.2 fusion.168
  57.3 0.3 fusion.169
  57.7 0.2 fusion.168
  57.9 0.3 fusion.169
  58.4 0.3 convert_reduce_fusion.1
  58.7 0.7 copy.55
  59.4 0.2 fusion.106
  59.6 0.2 convolution_convert_fusion
  59.8 18.5 %all_gather.7 = bf16[64,32,32]{0,2,1:T(8,128)(2,1)S(1)} all-gather(bf16[64,2,32]{0,2,1:T(8,128)(2,1)S(1)} %slice.54), channel_id=1, replica_groups=mesh['groups'=2,'dap'=16] {'dap'}, dimensions={1}, use_global_device_ids=true | all-gather | bytes 139264 | tf_op jit(solution)/shard_map/all_gather | solution.py:93
  78.3 0.3 fusion.72
  78.6 0.3 copy.54
  78.9 0.5 reshape.106
  79.5 0.8 fusion.77
  (48 shorter events, 0.6 us)
Async XLA Ops:
  0.6 2.0 %copy-start = (bf16[256,1024]{1,0:T(8,128)(2,1)S(1)}, bf16[256,1024]{1,0:T(8,128)(2,1)}, u32[]{:S(2)}) copy-start(bf16[256,1024]{1,0:T(8,128)(2,1)} %param.18) | copy-start | bytes 1572868
  7.1 4.4 %copy-start.4 = (bf16[2,32,128]{2,1,0:T(8,128)(2,1)S(1)}, bf16[2,32,128]{2,1,0:T(8,128)(2,1)}, u32[]{:S(2)}) copy-start(bf16[2,32,128]{2,1,0:T(8,128)(2,1)} %param.15) | copy-start | bytes 49156
  7.1 4.7 %copy-start.9 = (bf16[128,8]{0,1:T(8,128)(2,1)S(1)}, bf16[128,8]{0,1:T(8,128)(2,1)}, u32[]{:S(2)}) copy-start(bf16[128,8]{0,1:T(8,128)(2,1)} %param.17) | copy-start | bytes 6148
  35.4 5.9 %copy-start.7 = (s32[32,256]{1,0:T(8,128)S(1)}, s32[32,256]{1,0:T(8,128)}, u32[]{:S(2)}) copy-start(s32[32,256]{1,0:T(8,128)} %param.16) | copy-start | bytes 98308
  35.4 5.9 %copy-start.1 = (bf16[4,32,256]{2,1,0:T(8,128)(2,1)S(1)}, bf16[4,32,256]{2,1,0:T(8,128)(2,1)}, u32[]{:S(2)}) copy-start(bf16[4,32,256]{2,1,0:T(8,128)(2,1)} %param.14) | copy-start | bytes 196612
  35.4 5.9 %copy-start.6 = (bf16[256,256]{1,0:T(8,128)(2,1)S(1)}, bf16[256,256]{1,0:T(8,128)(2,1)}, u32[]{:S(2)}) copy-start(bf16[256,256]{1,0:T(8,128)(2,1)} %param.19) | copy-start | bytes 393220
  39.7 13.2 %copy-start.2 = (bf16[256,1024]{1,0:T(8,128)(2,1)S(1)}, bf16[256,1024]{1,0:T(8,128)(2,1)}, u32[]{:S(2)}) copy-start(bf16[256,1024]{1,0:T(8,128)(2,1)} %param.20) | copy-start | bytes 1572868
  42.2 10.4 %all-to-all-start = ((bf16[4,32,256]{2,0,1:T(4,128)(2,1)}), bf16[4,32,256]{2,0,1:T(4,128)(2,1)S(1)}, u32[]{:S(2)}, u32[]{:S(2)}) async-start(bf16[4,32,256]{2,0,1:T(4,128)(2,1)} %copy.46), calls=%async_computation | async-start | bytes 131072 | tf_op jit(solution)/shard_map/all_to_all | solution.py:74
  53.4 4.9 %copy-start.5 = (bf16[256,256]{1,0:T(8,128)(2,1)S(1)}, bf16[256,256]{1,0:T(8,128)(2,1)}, u32[]{:S(2)}) copy-start(bf16[256,256]{1,0:T(8,128)(2,1)} %param.21) | copy-start | bytes 393220
  53.5 6.1 %copy-start.8 = (bf16[256,64]{0,1:T(8,128)(2,1)S(1)}, bf16[256,64]{0,1:T(8,128)(2,1)}, u32[]{:S(2)}) copy-start(bf16[256,64]{0,1:T(8,128)(2,1)} %param.22) | copy-start | bytes 98308
  58.3 21.2 %copy-start.3 = (bf16[1024,128]{1,0:T(8,128)(2,1)S(1)}, bf16[1024,128]{1,0:T(8,128)(2,1)}, u32[]{:S(2)}) copy-start(bf16[1024,128]{1,0:T(8,128)(2,1)} %param.23) | copy-start | bytes 786436
where the time goes:
time: 80.6 us; the launch traced here: 80.2 us
  blocking collectives  41.8 us (52%)
  matrix products  12.4 us (15%)
  local copies, waits for them, and re-layouts  9.33 us (12%)
  waiting for transfers between devices  6.85 us (8%)
  other arithmetic  5.33 us (7%)
  starting transfers between devices  3.5 us (4%)
  between operations  0.95 us (1%)
    all_gather x1, blocking collectives, shards(): bias = lax.all_gather(own_bias, 'dap', axis=1, tiled=True)  23.3 us
    all_gather x1, blocking collectives, shards(): whole = lax.all_gather(right, 'dap', axis=1, tiled=True)  18.5 us
    all_to_all x1, waiting for transfers between devices, shards(): lax.all_to_all(homolog_later, 'dap', split_axis=1, concat_axis=0, tiled=T...  6.85 us
    dot_general x16, matrix products, one_head(): jnp.einsum('bij,bjd->bid', weights, vh, preferred_element_type=jnp.float32)  5.53 us
    reshape x3, local copies, waits for them, and re-layouts, attend(): proj = proj.reshape(batch, length, 4, HEAD_NUMBER, HEAD_WIDTH)  5.46 us
    all_to_all x1, starting transfers between devices, shards(): lax.all_to_all(homolog_later, 'dap', split_axis=1, concat_axis=0, tiled=T...  3.5 us
    sub x16, matrix products, one_head(): weights = jax.nn.softmax(scores, axis=-1).astype(jnp.bfloat16)  3.4 us
  transfers between devices with their start and end apart: 1, of which 1 were waited for; matrix products, arithmetic and copies ran while one was open for 0% of the time, Pallas kernels for 0%

commit v1 on v0

--- a/solution.py
+++ b/solution.py
@@ -1,11 +1,18 @@
+import functools
+
 import jax
 import jax.numpy as jnp
 from jax import lax
+from jax.experimental import pallas as pl
+from jax.experimental.pallas import tpu as pltpu
 from jax.sharding import PartitionSpec as P
 
 HEAD_NUMBER = 8
 HEAD_WIDTH = 32
 FACTOR_FEATURES = 32
+LANES = 128
+BF16 = jnp.bfloat16
+F32 = jnp.float32
 
 
 def standardise_features(values):
@@ -46,7 +53,7 @@
     return jnp.einsum("blk,kc->blc", gated, w_out, preferred_element_type=jnp.float32)
 
 
-def shards(
+def general_shards(
     homolog_tensor,
     couple_tensor,
     horizontal_drop_filter,
@@ -102,7 +109,286 @@
     return (alignment_output, pair_output_state)
 
 
+def dot(a, b, ca=1, cb=0):
+    return lax.dot_general(a, b, (((ca,), (cb,)), ((), ())), preferred_element_type=F32)
+
+
+def iota(shape, axis):
+    return lax.broadcasted_iota(jnp.int32, shape, axis)
+
+
+def slot_device(me, slot, rounds):
+    out = jnp.zeros_like(slot) + me
+    for bit, mask in enumerate(rounds):
+        out = out ^ (((slot >> bit) & 1) * mask)
+    return out
+
+
+def residue_order(me, length, own):
+    half = length // 2
+    place = iota((length, length), 0)
+    other = (place >= half).astype(jnp.int32)
+    rest = place - other * half
+    parity = other ^ (me & 1)
+    residue = ((rest // own) * 2 + parity) * own + rest % own
+    return (iota((length, length), 1) == residue).astype(F32).astype(BF16)
+
+
+def softmax_attention(q, k, v, bias_t, rows, groups):
+    features = q.shape[1]
+    per = LANES // HEAD_WIDTH
+    head_of_lane = iota((rows, LANES), 1) // HEAD_WIDTH
+    masks = [head_of_lane == t for t in range(per)]
+    zero = jnp.zeros((rows, LANES), BF16)
+    out = []
+    for g in range(groups):
+        parts = []
+        for part in range(features // LANES):
+            lanes = slice(part * LANES, (part + 1) * LANES)
+            qh = q[g * rows : (g + 1) * rows, lanes]
+            kh = k[g * rows : (g + 1) * rows, lanes]
+            vh = v[g * rows : (g + 1) * rows, lanes]
+            spread = jnp.concatenate([jnp.where(m, qh, zero) for m in masks], axis=0)
+            scores = dot(kh, spread, 1, 1)
+            if bias_t is not None:
+                scores = scores + bias_t[:, part * per * rows : (part + 1) * per * rows]
+            top = jnp.max(scores, axis=0, keepdims=True)
+            e = jnp.exp(scores - top)
+            w = (e / jnp.sum(e, axis=0, keepdims=True)).astype(BF16)
+            o = dot(w, vh, 0, 0)
+            acc = o[:rows]
+            for t in range(1, per):
+                acc = jnp.where(masks[t], o[t * rows : (t + 1) * rows], acc)
+            parts.append(acc)
+        out.append(jnp.concatenate(parts, axis=1))
+    return jnp.concatenate(out, axis=0)
+
+
+def gated_attention(x, w_ref, wo_ref, bias_t, rows, groups):
+    features = x.shape[1]
+    normed = standardise_features(x).astype(BF16)
+    q = (dot(normed, w_ref[:, :features]) * HEAD_WIDTH ** (-0.5)).astype(BF16)
+    k = dot(normed, w_ref[:, features : 2 * features]).astype(BF16)
+    v = dot(normed, w_ref[:, 2 * features : 3 * features]).astype(BF16)
+    o = softmax_attention(q, k, v, bias_t, rows, groups)
+    gate = dot(normed, w_ref[:, 3 * features :])
+    gated = (jax.nn.sigmoid(gate) * o).astype(BF16)
+    return dot(gated, wo_ref[...])
+
+
+def start_kernel(own, me_ref, msa_ref, pair_ref, wb_ref, out_ref):
+    me = me_ref[0]
+    seqs, length, features = msa_ref.shape
+    order = residue_order(me, length, own)
+    for s in range(seqs):
+        out_ref[s * length : (s + 1) * length, :] = dot(order, msa_ref[s]).astype(BF16)
+    zn = standardise_features(pair_ref[...]).astype(BF16)
+    bias = dot(wb_ref[...], zn, 0, 1)
+    pad = features - bias.shape[1]
+    block = jnp.concatenate([bias, jnp.zeros((bias.shape[0], pad), F32)], axis=1)
+    tail = out_ref.shape[0] - seqs * length - bias.shape[0]
+    block = jnp.concatenate([block, jnp.zeros((tail, features), F32)], axis=0)
+    out_ref[seqs * length :, :] = block.astype(BF16)
+
+
+def row_kernel(
+    rounds, seqs, own, me_ref, buf_ref, other_ref, w_ref, wo_ref, drop_ref, mine_ref, send_ref, acc_ref
+):
+    me = me_ref[0]
+    slots = buf_ref.shape[0]
+    length, features = drop_ref.shape
+    half = length // 2
+    order = residue_order(me, length, own)
+    blocks = [buf_ref[k, seqs * length : seqs * length + HEAD_NUMBER, :LANES] for k in range(slots)]
+    blocks += [other_ref[k] for k in range(slots)]
+    blocks = jnp.concatenate([b.astype(F32) for b in blocks], axis=0).astype(BF16)
+    shape = (2 * slots * HEAD_NUMBER, HEAD_NUMBER * length)
+    row = iota(shape, 0)
+    lane = iota(shape, 1)
+    slot = row // HEAD_NUMBER
+    cross = slot // slots
+    chip = slot_device(me, slot % slots, rounds) >> 1
+    base = (row % HEAD_NUMBER) * length + cross * half + chip * own
+    bias_t = None
+    for i in range(own):
+        place = (lane == base + i).astype(F32).astype(BF16)
+        part = dot(blocks, place, 0, 0)[i * length : (i + 1) * length]
+        bias_t = part if bias_t is None else bias_t + part
+    bias_t = dot(order, bias_t.astype(BF16))
+    drop = dot(order, drop_ref[...].astype(F32).astype(BF16)) * (1.0 / 0.9)
+
+    def body(t, carry):
+        both = [buf_ref[2 * t + u, : seqs * length, :] for u in range(2)]
+        x = jnp.concatenate(both, axis=0).astype(F32)
+        refresh = gated_attention(x, w_ref, wo_ref, bias_t, length, 2 * seqs)
+        tiled = jnp.concatenate([drop] * (2 * seqs), axis=0)
+        later = (x + tiled * refresh).astype(BF16)
+        size = 2 * seqs * length
+        later = later.astype(F32)
+        for part in range(features // LANES):
+            lanes = slice(part * LANES, (part + 1) * LANES)
+            acc_ref[part, pl.ds(pl.multiple_of(t * size, size), size), :] = later[:, lanes]
+        return carry
+
+    lax.fori_loop(0, slots // 2, body, 0)
+    count = slots * seqs
+    for r in range(length):
+        for part in range(features // LANES):
+            lanes = slice(part * LANES, (part + 1) * LANES)
+            rows = acc_ref[part, pl.ds(r, count, stride=length), :].astype(BF16)
+            if r < half:
+                mine_ref[r, :, lanes] = rows
+            else:
+                send_ref[r - half, :, lanes] = rows
+
+
+def column_kernel(
+    rounds,
+    seqs,
+    own,
+    me_ref,
+    mine_ref,
+    recv_ref,
+    w_ref,
+    wo_ref,
+    flanks_ref,
+    align_ref,
+    left_ref,
+    right_ref,
+    al_ref,
+    fac_ref,
+):
+    me = me_ref[0]
+    half, count, features = mine_ref.shape
+    total = 2 * count
+    group = 4
+
+    def body(t, carry):
+        pieces = []
+        for u in range(group):
+            pieces += [mine_ref[group * t + u], recv_ref[group * t + u]]
+        x = jnp.concatenate(pieces, axis=0).astype(F32)
+        refresh = gated_attention(x, w_ref, wo_ref, None, total, group)
+        aligned = (x + refresh).astype(BF16)
+        normed = standardise_features(aligned).astype(BF16)
+        factors = dot(normed, flanks_ref[...]).astype(BF16)
+        for u in range(group):
+            al_ref[group * t + u] = aligned[u * total : (u + 1) * total]
+            fac_ref[group * t + u] = factors[u * total : (u + 1) * total]
+            right_ref[group * t + u] = factors[u * total : (u + 1) * total, FACTOR_FEATURES:]
+        return carry
+
+    lax.fori_loop(0, half // group, body, 0)
+    place = iota((total, total), 1)
+    cross = place // count
+    within = place % count
+    device = slot_device(me, within // seqs, rounds) ^ cross
+    order = (iota((total, total), 0) == device * seqs + within % seqs).astype(F32).astype(BF16)
+    first = (me >> 1) * own
+    for i in range(own):
+        align_ref[i] = dot(order, al_ref[first + i]).astype(BF16)
+        left_ref[i] = fac_ref[first + i][:, :FACTOR_FEATURES]
+
+
+def small_shards(
+    devices,
+    homolog_tensor,
+    couple_tensor,
+    horizontal_drop_filter,
+    couple_offset_matrix,
+    horizontal_attend_matrix,
+    horizontal_exit_matrix,
+    vertical_attend_matrix,
+    vertical_exit_matrix,
+    averaged_product_flanks,
+    averaged_product_exit,
+):
+    seqs, length, features = homolog_tensor.shape
+    own = couple_tensor.shape[0]
+    channels = couple_tensor.shape[2]
+    half = length // 2
+    slots = devices // 2
+    count = slots * seqs
+    total = 2 * count
+    me = lax.axis_index("dap").astype(jnp.int32)
+    me_arr = me.reshape(1)
+    smem = pl.BlockSpec(memory_space=pltpu.SMEM)
+    vmem = pl.BlockSpec(memory_space=pltpu.VMEM)
+    rounds = []
+    mask = devices // 2
+    while mask > 1:
+        rounds.append(mask)
+        mask //= 2
+
+    def swap(x, by):
+        return lax.ppermute(x, "dap", [(i, i ^ by) for i in range(devices)])
+
+    height = seqs * length + 16
+    buf = pl.pallas_call(
+        functools.partial(start_kernel, own),
+        out_shape=jax.ShapeDtypeStruct((height, features), BF16),
+        in_specs=[smem, vmem, vmem, vmem],
+        out_specs=vmem,
+    )(me_arr, homolog_tensor, couple_tensor.reshape(own * length, channels), couple_offset_matrix)
+    buf = buf[None]
+    for by in rounds:
+        buf = jnp.concatenate([buf, swap(buf, by)], axis=0)
+    other = swap(buf[:, seqs * length : seqs * length + HEAD_NUMBER, :LANES], 1)
+    mine, send = pl.pallas_call(
+        functools.partial(row_kernel, tuple(rounds), seqs, own),
+        out_shape=[jax.ShapeDtypeStruct((half, count, features), BF16)] * 2,
+        in_specs=[smem] + [vmem] * 5,
+        out_specs=[vmem, vmem],
+        scratch_shapes=[pltpu.VMEM((features // LANES, count * length, LANES), F32)],
+    )(me_arr, buf, other, horizontal_attend_matrix, horizontal_exit_matrix, horizontal_drop_filter)
+    recv = swap(send, 1)
+    align, left, right = pl.pallas_call(
+        functools.partial(column_kernel, tuple(rounds), seqs, own),
+        out_shape=[
+            jax.ShapeDtypeStruct((own, total, features), BF16),
+            jax.ShapeDtypeStruct((own, total, FACTOR_FEATURES), BF16),
+            jax.ShapeDtypeStruct((half, total, FACTOR_FEATURES), BF16),
+        ],
+        in_specs=[smem] + [vmem] * 5,
+        out_specs=[vmem] * 3,
+        scratch_shapes=[
+            pltpu.VMEM((half, total, features), BF16),
+            pltpu.VMEM((half, total, 2 * FACTOR_FEATURES), BF16),
+        ],
+    )(me_arr, mine, recv, vertical_attend_matrix, vertical_exit_matrix, averaged_product_flanks)
+    alignment_output = jnp.swapaxes(align, 0, 1)
+    right_other = swap(right, 1)
+    right_other = jnp.concatenate([right_other[:, count:], right_other[:, :count]], axis=1)
+
+    def change_of(factor):
+        outer = jnp.einsum("isc,jsd->ijcd", left, factor, preferred_element_type=F32) / total
+        outer = outer.astype(BF16).reshape(own, half, FACTOR_FEATURES * FACTOR_FEATURES)
+        return jnp.einsum("ijk,kz->ijz", outer, averaged_product_exit, preferred_element_type=F32)
+
+    mine_change = change_of(right)
+    other_change = change_of(right_other)
+    odd = (me & 1) == 1
+    even_part = jnp.where(odd, other_change, mine_change).reshape(own, slots, 1, own, channels)
+    odd_part = jnp.where(odd, mine_change, other_change).reshape(own, slots, 1, own, channels)
+    change = jnp.concatenate([even_part, odd_part], axis=2).reshape(own, length, channels)
+    pair_output_state = (couple_tensor.astype(F32) + change).astype(BF16)
+    return (alignment_output, pair_output_state)
+
+
 def solution(mesh):
+    devices = mesh.shape["dap"]
+
+    def shards(homolog_tensor, couple_tensor, *rest):
+        seqs, length, features = homolog_tensor.shape
+        own = couple_tensor.shape[0]
+        power = devices >= 8 and devices & (devices - 1) == 0
+        fits = devices * seqs <= 64 and length <= 32 and features % LANES == 0
+        exact = own * devices == length and (own * length) <= LANES and (length // 2) % 4 == 0
+        aligned = length % 16 == 0 and (devices // 2 * seqs) % 16 == 0
+        if power and fits and exact and aligned:
+            return small_shards(devices, homolog_tensor, couple_tensor, *rest)
+        return general_shards(homolog_tensor, couple_tensor, *rest)
+
     placed = (
         P(("groups", "dap"), None, None),
         P(("groups", "dap"), None, None),

time: 80.6 us -> 65.8 us (0.82)
  blocking collectives: 41.8 us -> 0 us
  Pallas kernels: 0 us -> 30.9 us
  matrix products: 12.4 us -> 1.75 us
  waiting for transfers between devices: 6.85 us -> 15.7 us
  other arithmetic: 5.33 us -> 1.62 us
  starting transfers between devices: 3.5 us -> 6.97 us
  local copies, waits for them, and re-layouts: 9.33 us -> 7.23 us
    all_gather x2 -> x0, blocking collectives: 41.8 us -> none  [the longest x1 23.3 us: shards(): bias = lax.all_gather(own_bias, 'dap', axis=1, tiled=True)]
    pallas_call x0 -> x3, Pallas kernels: none -> 30.9 us  [the longest x1 20.3 us: small_shards(): pl.pallas_call(functools.partial(row_kernel, tuple(rounds), seqs, own), o...]
    ppermute x0 -> x6, waiting for transfers between devices: none -> 15.7 us  [swap(): return lax.ppermute(x, 'dap', [(i, i ^ by) for i in range(devices)])]
    dot_general x24 -> x4, matrix products: 9.02 us -> 1.75 us  [the longest x2 1.45 us: change_of(): jnp.einsum('isc,jsd->ijcd', left, factor, preferred_element_type=F32)]
    ppermute x0 -> x6, starting transfers between devices: none -> 6.97 us  [swap(): return lax.ppermute(x, 'dap', [(i, i ^ by) for i in range(devices)])]
    all_to_all x1 -> x0, waiting for transfers between devices: 6.85 us -> none  [shards(): lax.all_to_all(homolog_later, 'dap', split_axis=1, concat_axis=0, tiled=T...]
    reshape x5 -> x2, local copies, waits for them, and re-layouts: 6.17 us -> 0.56 us  [change_of(): outer.astype(BF16).reshape(own, half, FACTOR_FEATURES * FACTOR_FEATURES)]
    unnamed x21 -> x23, local copies, waits for them, and re-layouts: 0.76 us -> 6.29 us
  transfers between devices with their start and end apart: 1 -> 6, of which waited for: 1 -> 5; matrix products, arithmetic and copies ran while one was open for 0% -> 5% of each run, Pallas kernels for 0% -> 0%
where the time goes in v1:
time: 65.8 us; the launch traced here: 64.9 us
  Pallas kernels  30.9 us (47%)
  waiting for transfers between devices  15.7 us (24%)
  local copies, waits for them, and re-layouts  7.23 us (11%)
  starting transfers between devices  6.97 us (11%)
  matrix products  1.75 us (3%)
  other arithmetic  1.62 us (2%)
  between operations  0.78 us (1%)
    pallas_call x1, Pallas kernels, small_shards(): pl.pallas_call(functools.partial(row_kernel, tuple(rounds), seqs, own), o...  20.3 us
    ppermute x6, waiting for transfers between devices, swap(): return lax.ppermute(x, 'dap', [(i, i ^ by) for i in range(devices)])  15.7 us
    pallas_call x1, Pallas kernels, small_shards(): pl.pallas_call(functools.partial(column_kernel, tuple(rounds), seqs, own)...  8.75 us
    ppermute x6, starting transfers between devices, swap(): return lax.ppermute(x, 'dap', [(i, i ^ by) for i in range(devices)])  6.97 us
    unnamed x23, local copies, waits for them, and re-layouts  6.29 us
    pallas_call x1, Pallas kernels, small_shards(): pl.pallas_call(functools.partial(start_kernel, own), out_shape=jax.ShapeD...  1.79 us
    dot_general x2, matrix products, change_of(): jnp.einsum('isc,jsd->ijcd', left, factor, preferred_element_type=F32)  1.45 us
  transfers between devices with their start and end apart: 6, of which 5 were waited for; matrix products, arithmetic and copies ran while one was open for 5% of the time, Pallas kernels for 0%

profile of v1, /device:TPU:0, one launch (start us, length us, event | category | flops | bytes accessed | tf_op | source)
XLA Modules:
  0.0 64.9 jit_solution(11869890243658199846)
XLA Ops:
  0.6 0.0 copy-start
  0.6 0.0 copy-start.9
  0.7 0.7 %copy-done.9 = bf16[128,8]{0,1:T(8,128)(2,1)S(1)} copy-done((bf16[128,8]{0,1:T(8,128)(2,1)S(1)}, bf16[128,8]{0,1:T(8,128)(2,1)}, u32[]{:S(2)}) %copy-start.9) | copy-done | bytes 2072
  1.4 0.7 %copy.20.wb_ref = bf16[128,8]{1,0:T(8,128)(2,1)} copy(bf16[128,8]{0,1:T(8,128)(2,1)S(1)} %copy-done.9) | data formatting | bytes 4096 | tf_op args[3]
  2.1 1.8 %shard_map.113 = bf16[144,256]{1,0:T(8,128)(2,1)} custom-call(s32[1]{0:T(128)} %bitcast.me_ref, bf16[4,32,256]{2,1,0:T(8,128)(2,1)} %msa_ref.1, bf16[64,128]{1,0:T(8,128)(2,1)} %bitcast.46, bf16[128,8]{1,0:T(8,128)(2,1)} %copy.20.wb_ref), custom_call_target="tpu_custom_call" | custom-call | tf_op jit(solution)/shard_map/pallas_call | solution.py:327
  3.9 0.0 copy-start.2
  3.9 4.1 %collective-permute-start = (bf16[1,144,256]{2,1,0:T(8,128)(2,1)}, bf16[1,144,256]{2,1,0:T(8,128)(2,1)S(1)}, u32[]{:S(2)}, u32[]{:S(2)}) collective-permute-start(bf16[1,144,256]{2,1,0:T(8,128)(2,1)} %bitcast.40), channel_id=1, source_target_pairs={{0,8},{1,9},{2,10},{3,11},{4,12},{5,13},{6,14},{7,15},{8,0},{9,1},... | collective-permute-start | bytes 221192 | tf_op jit(solution)/shard_map/ppermute | solution.py:324
  8.0 4.2 %collective-permute-done = bf16[1,144,256]{2,1,0:T(8,128)(2,1)S(1)} collective-permute-done((bf16[1,144,256]{2,1,0:T(8,128)(2,1)}, bf16[1,144,256]{2,1,0:T(8,128)(2,1)S(1)}, u32[]{:S(2)}, u32[]{:S(2)}) %collective-permute-start) | collective-permute-done | bytes 73760 | tf_op jit(solution)/shard_map/ppermute | solution.py:324
  12.1 0.9 %pad_maximum_fusion.2 = bf16[2,144,256]{2,1,0:T(8,128)(2,1)S(1)} fusion(bf16[1,144,256]{2,1,0:T(8,128)(2,1)S(1)} %collective-permute-done, bf16[1,144,256]{2,1,0:T(8,128)(2,1)} %bitcast.41), kind=kLoop, calls=%fused_computation.16 | loop fusion | flops 73728 | bytes 294912 | tf_op jit(solution)/shard_map/concatenate | solution.py:335
  13.0 0.8 %collective-permute-start.1 = (bf16[2,144,256]{2,1,0:T(8,128)(2,1)S(1)}, bf16[2,144,256]{2,1,0:T(8,128)(2,1)S(1)}, u32[]{:S(2)}, u32[]{:S(2)}) collective-permute-start(bf16[2,144,256]{2,1,0:T(8,128)(2,1)S(1)} %pad_maximum_fusion.2), channel_id=1, source_target_pairs={{0,4},{1,5},{2,6},{3,7},{4,0},{5,1},{6,2},{7,3},{8,12},{9,13},{10,... | collective-permute-start | bytes 442376 | tf_op jit(solution)/shard_map/ppermute | solution.py:324
  13.8 4.4 %collective-permute-done.1 = bf16[2,144,256]{2,1,0:T(8,128)(2,1)S(1)} collective-permute-done((bf16[2,144,256]{2,1,0:T(8,128)(2,1)S(1)}, bf16[2,144,256]{2,1,0:T(8,128)(2,1)S(1)}, u32[]{:S(2)}, u32[]{:S(2)}) %collective-permute-start.1) | collective-permute-done | bytes 147488 | tf_op jit(solution)/shard_map/ppermute | solution.py:324
  18.3 0.0 copy-done.2
  18.3 1.7 %collective-permute-start.2 = (bf16[4,144,256]{2,1,0:T(8,128)(2,1)S(1)}, bf16[4,144,256]{2,1,0:T(8,128)(2,1)S(1)}, u32[]{:S(2)}, u32[]{:S(2)}) collective-permute-start(bf16[4,144,256]{2,1,0:T(8,128)(2,1)S(1)} %pad_maximum_fusion.1), channel_id=1, source_target_pairs={{0,2},{1,3},{2,0},{3,1},{4,6},{5,7},{6,4},{7,5},{8,10},{9,11},{10,... | collective-permute-start | bytes 884744 | tf_op jit(solution)/shard_map/ppermute | solution.py:324
  20.0 5.0 %collective-permute-done.2 = bf16[4,144,256]{2,1,0:T(8,128)(2,1)S(1)} collective-permute-done((bf16[4,144,256]{2,1,0:T(8,128)(2,1)S(1)}, bf16[4,144,256]{2,1,0:T(8,128)(2,1)S(1)}, u32[]{:S(2)}, u32[]{:S(2)}) %collective-permute-start.2) | collective-permute-done | bytes 294944 | tf_op jit(solution)/shard_map/ppermute | solution.py:324
  25.1 0.1 pad_maximum_fusion.buf_ref
  25.1 0.0 copy-start.1
  25.2 0.0 copy-start.7
  25.2 0.1 collective-permute-start.3
  25.3 1.2 %collective-permute-done.3.other_ref = bf16[8,8,128]{2,1,0:T(8,128)(2,1)S(1)} collective-permute-done((bf16[8,8,128]{2,1,0:T(8,128)(2,1)S(1)}, bf16[8,8,128]{2,1,0:T(8,128)(2,1)S(1)}, u32[]{:S(2)}, u32[]{:S(2)}) %collective-permute-start.3) | collective-permute-done | bytes 16416 | tf_op jit(solution)/shard_map/ppermute | solution.py:324
  26.4 0.0 copy-done.1
  26.4 0.0 copy-start.8
  26.4 0.6 copy-done.8
  27.0 20.3 %shard_map.114 = (bf16[16,32,256]{2,1,0:T(8,128)(2,1)}, bf16[16,32,256]{2,1,0:T(8,128)(2,1)}) custom-call(s32[1]{0:T(128)} %bitcast.me_ref, bf16[8,144,256]{2,1,0:T(8,128)(2,1)} %copy-done.1, bf16[8,8,128]{2,1,0:T(8,128)(2,1)} %copy-done.8, bf16[256,1024]{1,0:T(8,128)(2,1)} %w_ref.2, bf16[256,256]{1,0:T(8,128)(2,1)} %wo_ref.2, s32[32,256]{1,0:T(8,128)} %drop_ref.1), custom_call_target="tpu_custom_call" | custom-call | tf_op jit(solution)/shard_map/pallas_call | solution.py:337
  47.4 0.2 collective-permute-start.4
  47.5 0.0 copy-done.7
  47.5 0.7 %copy.21.flanks_ref = bf16[256,64]{1,0:T(8,128)(2,1)} copy(bf16[256,64]{0,1:T(8,128)(2,1)S(1)} %copy-done.7) | data formatting | bytes 65536 | tf_op args[8]
  48.3 0.8 %collective-permute-done.4.recv_ref = bf16[16,32,256]{2,1,0:T(8,128)(2,1)S(1)} collective-permute-done((bf16[16,32,256]{2,1,0:T(8,128)(2,1)}, bf16[16,32,256]{2,1,0:T(8,128)(2,1)S(1)}, u32[]{:S(2)}, u32[]{:S(2)}) %collective-permute-start.4) | collective-permute-done | bytes 262176 | tf_op jit(solution)/shard_map/ppermute | solution.py:324
  49.1 0.0 copy-start.3
  49.1 0.7 %copy-done.3 = bf16[16,32,256]{2,1,0:T(8,128)(2,1)} copy-done((bf16[16,32,256]{2,1,0:T(8,128)(2,1)}, bf16[16,32,256]{2,1,0:T(8,128)(2,1)S(1)}, u32[]{:S(2)}) %copy-start.3) | copy-done | bytes 262168
  49.8 8.7 %shard_map.115 = (bf16[2,64,256]{2,1,0:T(8,128)(2,1)}, bf16[2,64,32]{2,1,0:T(8,128)(2,1)}, bf16[16,64,32]{2,1,0:T(8,128)(2,1)}) custom-call(s32[1]{0:T(128)} %bitcast.me_ref, bf16[16,32,256]{2,1,0:T(8,128)(2,1)} %get-tuple-element.7.mine_ref, bf16[16,32,256]{2,1,0:T(8,128)(2,1)} %copy-done.3, bf16[256,1024]{1,0:T(8,128)(2,1)} %w_ref.3, ...), custom_call_target="tpu_custom_call" | custom-call | tf_op jit(solution)/shard_map/pallas_call | solution.py:345
  58.6 0.2 collective-permute-start.5
  58.7 1.2 %fusion.2 = bf16[2,16,32,32]{2,3,0,1:T(8,128)(2,1)S(1)} fusion(bf16[16,64,32]{2,1,0:T(8,128)(2,1)} %get-tuple-element.10, bf16[2,64,32]{2,1,0:T(8,128)(2,1)} %get-tuple-element.11), kind=kOutput, calls=%fused_computation.4 | convolution fusion | flops 4259840 | bytes 139264 | tf_op jit(solution)/shard_map/isc,jsd->ijcd/dot_general | solution.py:364
  59.9 0.2 copy.27
  60.1 0.3 reshape.28
  60.4 0.0 copy-done
  60.4 0.0 copy-start.5
  60.4 0.2 fusion.7
  60.6 0.7 %copy-done.5 = bf16[2,64,256]{2,1,0:T(8,128)(2,1)S(1)} copy-done((bf16[2,64,256]{2,1,0:T(8,128)(2,1)S(1)}, bf16[2,64,256]{2,1,0:T(8,128)(2,1)}, u32[]{:S(2)}) %copy-start.5) | copy-done | bytes 65560
  61.2 0.7 %copy.29 = bf16[64,2,256]{2,1,0:T(2,128)(2,1)} copy(bf16[64,2,256]{2,0,1:T(8,128)(2,1)S(1)} %bitcast.45) | data formatting | bytes 131072
  61.9 0.0 copy-start.4
  61.9 0.0 collective-permute-done.5
  62.0 0.7 %copy-done.4 = bf16[2,64,32]{2,1,0:T(8,128)(2,1)S(1)} copy-done((bf16[2,64,32]{2,1,0:T(8,128)(2,1)S(1)}, bf16[2,64,32]{2,1,0:T(8,128)(2,1)}, u32[]{:S(2)}) %copy-start.4) | copy-done | bytes 8216
  62.7 0.2 fusion.3
  63.0 0.2 copy.24
  63.1 0.3 reshape.27
  63.4 0.2 broadcast_select_fusion.1
  63.6 0.0 copy-start.6
  63.6 0.7 %copy-done.6 = bf16[2,32,128]{2,1,0:T(8,128)(2,1)S(1)} copy-done((bf16[2,32,128]{2,1,0:T(8,128)(2,1)S(1)}, bf16[2,32,128]{2,1,0:T(8,128)(2,1)}, u32[]{:S(2)}) %copy-start.6) | copy-done | bytes 16408
  64.3 0.6 add_convert_fusion
  (5 shorter events, 0.1 us)
Async XLA Ops:
  0.6 59.8 %copy-start = (bf16[1024,128]{1,0:T(8,128)(2,1)S(1)}, bf16[1024,128]{1,0:T(8,128)(2,1)}, u32[]{:S(2)}) copy-start(bf16[1024,128]{1,0:T(8,128)(2,1)} %param.19) | copy-start | bytes 786436
  0.6 0.7 %copy-start.9 = (bf16[128,8]{0,1:T(8,128)(2,1)S(1)}, bf16[128,8]{0,1:T(8,128)(2,1)}, u32[]{:S(2)}) copy-start(bf16[128,8]{0,1:T(8,128)(2,1)} %param.13) | copy-start | bytes 6148
  3.9 14.4 %copy-start.2 = (bf16[144,256]{1,0:T(8,128)(2,1)S(1)}, bf16[144,256]{1,0:T(8,128)(2,1)}, u32[]{:S(2)}) copy-start(bf16[144,256]{1,0:T(8,128)(2,1)} %shard_map.113) | copy-start | bytes 221188
  3.9 8.3 %collective-permute-start = (bf16[1,144,256]{2,1,0:T(8,128)(2,1)}, bf16[1,144,256]{2,1,0:T(8,128)(2,1)S(1)}, u32[]{:S(2)}, u32[]{:S(2)}) collective-permute-start(bf16[1,144,256]{2,1,0:T(8,128)(2,1)} %bitcast.40), channel_id=1, source_target_pairs={{0,8},{1,9},{2,10},{3,11},{4,12},{5,13},{6,14},{7,15},{8,0},{9,1},... | collective-permute-start | bytes 221192 | tf_op jit(solution)/shard_map/ppermute | solution.py:324
  13.0 5.2 %collective-permute-start.1 = (bf16[2,144,256]{2,1,0:T(8,128)(2,1)S(1)}, bf16[2,144,256]{2,1,0:T(8,128)(2,1)S(1)}, u32[]{:S(2)}, u32[]{:S(2)}) collective-permute-start(bf16[2,144,256]{2,1,0:T(8,128)(2,1)S(1)} %pad_maximum_fusion.2), channel_id=1, source_target_pairs={{0,4},{1,5},{2,6},{3,7},{4,0},{5,1},{6,2},{7,3},{8,12},{9,13},{10,... | collective-permute-start | bytes 442376 | tf_op jit(solution)/shard_map/ppermute | solution.py:324
  18.3 6.8 %collective-permute-start.2 = (bf16[4,144,256]{2,1,0:T(8,128)(2,1)S(1)}, bf16[4,144,256]{2,1,0:T(8,128)(2,1)S(1)}, u32[]{:S(2)}, u32[]{:S(2)}) collective-permute-start(bf16[4,144,256]{2,1,0:T(8,128)(2,1)S(1)} %pad_maximum_fusion.1), channel_id=1, source_target_pairs={{0,2},{1,3},{2,0},{3,1},{4,6},{5,7},{6,4},{7,5},{8,10},{9,11},{10,... | collective-permute-start | bytes 884744 | tf_op jit(solution)/shard_map/ppermute | solution.py:324
  25.1 1.3 %copy-start.1 = (bf16[8,144,256]{2,1,0:T(8,128)(2,1)}, bf16[8,144,256]{2,1,0:T(8,128)(2,1)S(1)}, u32[]{:S(2)}) copy-start(bf16[8,144,256]{2,1,0:T(8,128)(2,1)S(1)} %pad_maximum_fusion.buf_ref) | copy-start | bytes 1769476
  25.2 22.4 %copy-start.7 = (bf16[256,64]{0,1:T(8,128)(2,1)S(1)}, bf16[256,64]{0,1:T(8,128)(2,1)}, u32[]{:S(2)}) copy-start(bf16[256,64]{0,1:T(8,128)(2,1)} %param.18) | copy-start | bytes 98308
  25.2 1.2 %collective-permute-start.3 = (bf16[8,8,128]{2,1,0:T(8,128)(2,1)S(1)}, bf16[8,8,128]{2,1,0:T(8,128)(2,1)S(1)}, u32[]{:S(2)}, u32[]{:S(2)}) collective-permute-start(bf16[8,8,128]{2,1,0:T(8,128)(2,1)S(1)} %slice.12), channel_id=1, source_target_pairs={{0,1},{1,0},{2,3},{3,2},{4,5},{5,4},{6,7},{7,6},{8,9},{9,8},{10,11... | collective-permute-start | bytes 49160 | tf_op jit(solution)/shard_map/ppermute | solution.py:324
  26.4 0.6 copy-start.8
  47.4 1.7 %collective-permute-start.4 = (bf16[16,32,256]{2,1,0:T(8,128)(2,1)}, bf16[16,32,256]{2,1,0:T(8,128)(2,1)S(1)}, u32[]{:S(2)}, u32[]{:S(2)}) collective-permute-start(bf16[16,32,256]{2,1,0:T(8,128)(2,1)} %get-tuple-element.8), channel_id=1, source_target_pairs={{0,1},{1,0},{2,3},{3,2},{4,5},{5,4},{6,7},{7,6},{8,9},{9,8},{10,11... | collective-permute-start | bytes 786440 | tf_op jit(solution)/shard_map/ppermute | solution.py:324
  49.1 0.7 %copy-start.3 = (bf16[16,32,256]{2,1,0:T(8,128)(2,1)}, bf16[16,32,256]{2,1,0:T(8,128)(2,1)S(1)}, u32[]{:S(2)}) copy-start(bf16[16,32,256]{2,1,0:T(8,128)(2,1)S(1)} %collective-permute-done.4.recv_ref) | copy-start | bytes 786436
  58.6 3.4 %collective-permute-start.5 = (bf16[16,64,32]{2,1,0:T(8,128)(2,1)}, bf16[16,64,32]{2,1,0:T(8,128)(2,1)S(1)}, u32[]{:S(2)}, u32[]{:S(2)}) collective-permute-start(bf16[16,64,32]{2,1,0:T(8,128)(2,1)} %get-tuple-element.10), channel_id=1, source_target_pairs={{0,1},{1,0},{2,3},{3,2},{4,5},{5,4},{6,7},{7,6},{8,9},{9,8},{10,11... | collective-permute-start | bytes 196616 | tf_op jit(solution)/shard_map/ppermute | solution.py:324
  60.4 0.8 %copy-start.5 = (bf16[2,64,256]{2,1,0:T(8,128)(2,1)S(1)}, bf16[2,64,256]{2,1,0:T(8,128)(2,1)}, u32[]{:S(2)}) copy-start(bf16[2,64,256]{2,1,0:T(8,128)(2,1)} %get-tuple-element.9) | copy-start | bytes 196612
  61.9 0.8 %copy-start.4 = (bf16[2,64,32]{2,1,0:T(8,128)(2,1)S(1)}, bf16[2,64,32]{2,1,0:T(8,128)(2,1)}, u32[]{:S(2)}) copy-start(bf16[2,64,32]{2,1,0:T(8,128)(2,1)} %get-tuple-element.11) | copy-start | bytes 24580
  63.6 0.7 %copy-start.6 = (bf16[2,32,128]{2,1,0:T(8,128)(2,1)S(1)}, bf16[2,32,128]{2,1,0:T(8,128)(2,1)}, u32[]{:S(2)}) copy-start(bf16[2,32,128]{2,1,0:T(8,128)(2,1)} %param.11) | copy-start | bytes 49156

commit v2 on v1

--- a/solution.py
+++ b/solution.py
@@ -140,28 +140,34 @@
     head_of_lane = iota((rows, LANES), 1) // HEAD_WIDTH
     masks = [head_of_lane == t for t in range(per)]
     zero = jnp.zeros((rows, LANES), BF16)
-    out = []
-    for g in range(groups):
-        parts = []
-        for part in range(features // LANES):
-            lanes = slice(part * LANES, (part + 1) * LANES)
-            qh = q[g * rows : (g + 1) * rows, lanes]
-            kh = k[g * rows : (g + 1) * rows, lanes]
-            vh = v[g * rows : (g + 1) * rows, lanes]
-            spread = jnp.concatenate([jnp.where(m, qh, zero) for m in masks], axis=0)
-            scores = dot(kh, spread, 1, 1)
-            if bias_t is not None:
-                scores = scores + bias_t[:, part * per * rows : (part + 1) * per * rows]
-            top = jnp.max(scores, axis=0, keepdims=True)
-            e = jnp.exp(scores - top)
-            w = (e / jnp.sum(e, axis=0, keepdims=True)).astype(BF16)
-            o = dot(w, vh, 0, 0)
-            acc = o[:rows]
-            for t in range(1, per):
-                acc = jnp.where(masks[t], o[t * rows : (t + 1) * rows], acc)
-            parts.append(acc)
-        out.append(jnp.concatenate(parts, axis=1))
-    return jnp.concatenate(out, axis=0)
+    units = [(g, part) for g in range(groups) for part in range(features // LANES)]
+
+    def piece(x, unit):
+        g, part = unit
+        return x[g * rows : (g + 1) * rows, part * LANES : (part + 1) * LANES]
+
+    scores = []
+    for unit in units:
+        qh = piece(q, unit)
+        spread = jnp.concatenate([jnp.where(m, qh, zero) for m in masks], axis=0)
+        scores.append(dot(piece(k, unit), spread, 1, 1))
+    scores = jnp.concatenate(scores, axis=1)
+    if bias_t is not None:
+        scores = scores + jnp.concatenate([bias_t] * groups, axis=1)
+    e = jnp.exp(scores - jnp.max(scores, axis=0, keepdims=True))
+    w = (e * (1.0 / jnp.sum(e, axis=0, keepdims=True))).astype(BF16)
+    width = per * rows
+    parts = []
+    for n, unit in enumerate(units):
+        o = dot(w[:, n * width : (n + 1) * width], piece(v, unit), 0, 0)
+        acc = o[:rows]
+        for t in range(1, per):
+            acc = jnp.where(masks[t], o[t * rows : (t + 1) * rows], acc)
+        parts.append(acc)
+    count = features // LANES
+    return jnp.concatenate(
+        [jnp.concatenate(parts[g * count : (g + 1) * count], axis=1) for g in range(groups)], axis=0
+    )
 
 
 def gated_attention(x, w_ref, wo_ref, bias_t, rows, groups):
@@ -217,29 +223,24 @@
     bias_t = dot(order, bias_t.astype(BF16))
     drop = dot(order, drop_ref[...].astype(F32).astype(BF16)) * (1.0 / 0.9)
 
+    batch = 2 * seqs
+    size = batch * length
+    row = iota((size, size), 0)
+    turn = (iota((size, size), 1) == (row % batch) * length + row // batch).astype(F32).astype(BF16)
+
     def body(t, carry):
         both = [buf_ref[2 * t + u, : seqs * length, :] for u in range(2)]
         x = jnp.concatenate(both, axis=0).astype(F32)
-        refresh = gated_attention(x, w_ref, wo_ref, bias_t, length, 2 * seqs)
-        tiled = jnp.concatenate([drop] * (2 * seqs), axis=0)
+        refresh = gated_attention(x, w_ref, wo_ref, bias_t, length, batch)
+        tiled = jnp.concatenate([drop] * batch, axis=0)
         later = (x + tiled * refresh).astype(BF16)
-        size = 2 * seqs * length
-        later = later.astype(F32)
-        for part in range(features // LANES):
-            lanes = slice(part * LANES, (part + 1) * LANES)
-            acc_ref[part, pl.ds(pl.multiple_of(t * size, size), size), :] = later[:, lanes]
+        turned = dot(turn, later).reshape(length, batch, features)
+        acc_ref[:, pl.ds(pl.multiple_of(t * batch, batch), batch), :] = turned
         return carry
 
     lax.fori_loop(0, slots // 2, body, 0)
-    count = slots * seqs
-    for r in range(length):
-        for part in range(features // LANES):
-            lanes = slice(part * LANES, (part + 1) * LANES)
-            rows = acc_ref[part, pl.ds(r, count, stride=length), :].astype(BF16)
-            if r < half:
-                mine_ref[r, :, lanes] = rows
-            else:
-                send_ref[r - half, :, lanes] = rows
+    mine_ref[...] = acc_ref[:half].astype(BF16)
+    send_ref[...] = acc_ref[half:].astype(BF16)
 
 
 def column_kernel(
@@ -314,6 +315,7 @@
     me_arr = me.reshape(1)
     smem = pl.BlockSpec(memory_space=pltpu.SMEM)
     vmem = pl.BlockSpec(memory_space=pltpu.VMEM)
+    params = pltpu.CompilerParams(vmem_limit_bytes=24 * 1024 * 1024)
     rounds = []
     mask = devices // 2
     while mask > 1:
@@ -329,6 +331,7 @@
         out_shape=jax.ShapeDtypeStruct((height, features), BF16),
         in_specs=[smem, vmem, vmem, vmem],
         out_specs=vmem,
+        compiler_params=params,
     )(me_arr, homolog_tensor, couple_tensor.reshape(own * length, channels), couple_offset_matrix)
     buf = buf[None]
     for by in rounds:
@@ -339,7 +342,8 @@
         out_shape=[jax.ShapeDtypeStruct((half, count, features), BF16)] * 2,
         in_specs=[smem] + [vmem] * 5,
         out_specs=[vmem, vmem],
-        scratch_shapes=[pltpu.VMEM((features // LANES, count * length, LANES), F32)],
+        scratch_shapes=[pltpu.VMEM((length, count, features), F32)],
+        compiler_params=params,
     )(me_arr, buf, other, horizontal_attend_matrix, horizontal_exit_matrix, horizontal_drop_filter)
     recv = swap(send, 1)
     align, left, right = pl.pallas_call(
@@ -355,6 +359,7 @@
             pltpu.VMEM((half, total, features), BF16),
             pltpu.VMEM((half, total, 2 * FACTOR_FEATURES), BF16),
         ],
+        compiler_params=params,
     )(me_arr, mine, recv, vertical_attend_matrix, vertical_exit_matrix, averaged_product_flanks)
     alignment_output = jnp.swapaxes(align, 0, 1)
     right_other = swap(right, 1)

time: 65.8 us -> 42.2 us (0.64)
  Pallas kernels: 30.9 us -> 12 us
  local copies, waits for them, and re-layouts: 7.23 us -> 4.08 us
  matrix products: 1.75 us -> 0.81 us
  other arithmetic: 1.62 us -> 0.74 us
    pallas_call x1, Pallas kernels: 20.3 us -> 5.85 us  [small_shards(): pl.pallas_call(functools.partial(row_kernel, tuple(rounds), seqs, own), o...]
    unnamed x23, local copies, waits for them, and re-layouts: 6.29 us -> 3.14 us
    pallas_call x1, Pallas kernels: 8.75 us -> 5.83 us  [small_shards(): pl.pallas_call(functools.partial(column_kernel, tuple(rounds), seqs, own)...]
    pallas_call x1, Pallas kernels: 1.79 us -> 0.3 us  [small_shards(): pl.pallas_call(functools.partial(start_kernel, own), out_shape=jax.ShapeD...]
    dot_general x2, matrix products: 1.45 us -> 0.5 us  [change_of(): jnp.einsum('isc,jsd->ijcd', left, factor, preferred_element_type=F32)]
    concatenate x3, other arithmetic: 0.99 us -> 0.11 us  [small_shards(): buf = jnp.concatenate([buf, swap(buf, by)], axis=0)]
  transfers between devices with their start and end apart: 6 -> 6, of which waited for: 5 -> 5; matrix products, arithmetic and copies ran while one was open for 5% -> 4% of each run, Pallas kernels for 0% -> 0%
where the time goes in v2:
time: 42.2 us; the launch traced here: 41.4 us
  waiting for transfers between devices  15.8 us (37%)
  Pallas kernels  12 us (28%)
  starting transfers between devices  7.12 us (17%)
  local copies, waits for them, and re-layouts  4.08 us (10%)
  between operations  0.82 us (2%)
  matrix products  0.81 us (2%)
  other arithmetic  0.74 us (2%)
    ppermute x6, waiting for transfers between devices, swap(): return lax.ppermute(x, 'dap', [(i, i ^ by) for i in range(devices)])  15.8 us
    ppermute x6, starting transfers between devices, swap(): return lax.ppermute(x, 'dap', [(i, i ^ by) for i in range(devices)])  7.12 us
    pallas_call x1, Pallas kernels, small_shards(): pl.pallas_call(functools.partial(row_kernel, tuple(rounds), seqs, own), o...  5.85 us
    pallas_call x1, Pallas kernels, small_shards(): pl.pallas_call(functools.partial(column_kernel, tuple(rounds), seqs, own)...  5.83 us
    unnamed x23, local copies, waits for them, and re-layouts  3.14 us
  transfers between devices with their start and end apart: 6, of which 5 were waited for; matrix products, arithmetic and copies ran while one was open for 4% of the time, Pallas kernels for 0%

profile of v2, /device:TPU:0, one launch (start us, length us, event | category | flops | bytes accessed | tf_op | source)
XLA Modules:
  0.0 41.4 jit_solution(13049734683894042428)
XLA Ops:
  0.6 0.0 copy-start
  0.6 0.0 copy-start.9
  0.7 0.7 %copy-done.9 = bf16[128,8]{0,1:T(8,128)(2,1)S(1)} copy-done((bf16[128,8]{0,1:T(8,128)(2,1)S(1)}, bf16[128,8]{0,1:T(8,128)(2,1)}, u32[]{:S(2)}) %copy-start.9) | copy-done | bytes 2072
  1.4 0.0 copy-start.6
  1.4 0.1 copy.20.wb_ref
  1.5 0.6 %copy-done.6 = bf16[2,32,128]{2,1,0:T(8,128)(2,1)S(1)} copy-done((bf16[2,32,128]{2,1,0:T(8,128)(2,1)S(1)}, bf16[2,32,128]{2,1,0:T(8,128)(2,1)}, u32[]{:S(2)}) %copy-start.6) | copy-done | bytes 16408
  2.1 0.0 copy-start.5
  2.1 0.8 %copy-done.5 = bf16[4,32,256]{2,1,0:T(8,128)(2,1)S(1)} copy-done((bf16[4,32,256]{2,1,0:T(8,128)(2,1)S(1)}, bf16[4,32,256]{2,1,0:T(8,128)(2,1)}, u32[]{:S(2)}) %copy-start.5) | copy-done | bytes 65560
  2.9 0.3 shard_map.113
  3.2 4.1 %collective-permute-start = (bf16[1,144,256]{2,1,0:T(8,128)(2,1)S(1)}, bf16[1,144,256]{2,1,0:T(8,128)(2,1)S(1)}, u32[]{:S(2)}, u32[]{:S(2)}) collective-permute-start(bf16[1,144,256]{2,1,0:T(8,128)(2,1)S(1)} %bitcast.40), channel_id=1, source_target_pairs={{0,8},{1,9},{2,10},{3,11},{4,12},{5,13},{6,14},{7,15},{8,0},{9,1},... | collective-permute-start | bytes 221192 | tf_op jit(solution)/shard_map/ppermute | solution.py:326
  7.3 3.9 %collective-permute-done = bf16[1,144,256]{2,1,0:T(8,128)(2,1)S(1)} collective-permute-done((bf16[1,144,256]{2,1,0:T(8,128)(2,1)S(1)}, bf16[1,144,256]{2,1,0:T(8,128)(2,1)S(1)}, u32[]{:S(2)}, u32[]{:S(2)}) %collective-permute-start) | collective-permute-done | bytes 73760 | tf_op jit(solution)/shard_map/ppermute | solution.py:326
  11.2 0.7 %collective-permute-start.1 = (bf16[2,144,256]{2,1,0:T(8,128)(2,1)S(1)}, bf16[2,144,256]{2,1,0:T(8,128)(2,1)S(1)}, u32[]{:S(2)}, u32[]{:S(2)}) collective-permute-start(bf16[2,144,256]{2,1,0:T(8,128)(2,1)S(1)} %pad_maximum_fusion.2), channel_id=1, source_target_pairs={{0,4},{1,5},{2,6},{3,7},{4,0},{5,1},{6,2},{7,3},{8,12},{9,13},{10,... | collective-permute-start | bytes 442376 | tf_op jit(solution)/shard_map/ppermute | solution.py:326
  12.0 4.5 %collective-permute-done.1 = bf16[2,144,256]{2,1,0:T(8,128)(2,1)S(1)} collective-permute-done((bf16[2,144,256]{2,1,0:T(8,128)(2,1)S(1)}, bf16[2,144,256]{2,1,0:T(8,128)(2,1)S(1)}, u32[]{:S(2)}, u32[]{:S(2)}) %collective-permute-start.1) | collective-permute-done | bytes 147488 | tf_op jit(solution)/shard_map/ppermute | solution.py:326
  16.5 0.0 copy-start.1
  16.5 0.0 copy-start.3
  16.5 1.8 %collective-permute-start.2 = (bf16[4,144,256]{2,1,0:T(8,128)(2,1)S(1)}, bf16[4,144,256]{2,1,0:T(8,128)(2,1)S(1)}, u32[]{:S(2)}, u32[]{:S(2)}) collective-permute-start(bf16[4,144,256]{2,1,0:T(8,128)(2,1)S(1)} %pad_maximum_fusion.1), channel_id=1, source_target_pairs={{0,2},{1,3},{2,0},{3,1},{4,6},{5,7},{6,4},{7,5},{8,10},{9,11},{10,... | collective-permute-start | bytes 884744 | tf_op jit(solution)/shard_map/ppermute | solution.py:326
  18.3 5.0 %collective-permute-done.2 = bf16[4,144,256]{2,1,0:T(8,128)(2,1)S(1)} collective-permute-done((bf16[4,144,256]{2,1,0:T(8,128)(2,1)S(1)}, bf16[4,144,256]{2,1,0:T(8,128)(2,1)S(1)}, u32[]{:S(2)}, u32[]{:S(2)}) %collective-permute-start.2) | collective-permute-done | bytes 294944 | tf_op jit(solution)/shard_map/ppermute | solution.py:326
  23.3 0.1 pad_maximum_fusion.buf_ref
  23.3 0.0 copy-start.7
  23.4 0.0 copy-start.8
  23.4 0.0 copy-start.2
  23.4 0.1 collective-permute-start.3
  23.5 1.2 %collective-permute-done.3.other_ref = bf16[8,8,128]{2,1,0:T(8,128)(2,1)S(1)} collective-permute-done((bf16[8,8,128]{2,1,0:T(8,128)(2,1)S(1)}, bf16[8,8,128]{2,1,0:T(8,128)(2,1)S(1)}, u32[]{:S(2)}, u32[]{:S(2)}) %collective-permute-start.3) | collective-permute-done | bytes 16416 | tf_op jit(solution)/shard_map/ppermute | solution.py:326
  24.6 0.0 copy-done.1
  24.6 0.0 copy-done.3
  24.7 0.0 copy-done.7
  24.7 0.0 copy-start.4
  24.7 5.8 %shard_map.114 = (bf16[16,32,256]{2,1,0:T(8,128)(2,1)S(1)}, bf16[16,32,256]{2,1,0:T(8,128)(2,1)S(1)}) custom-call(s32[1]{0:T(128)} %bitcast.me_ref, bf16[8,144,256]{2,1,0:T(8,128)(2,1)S(1)} %pad_maximum_fusion.buf_ref, bf16[8,8,128]{2,1,0:T(8,128)(2,1)S(1)} %collective-permute-done.3.other_ref, bf16[256,1024]{1,0:T(8,128)(2,1)S(1)} %copy-done.1, ...), custom_call_target="tpu_custom_call" | custom-call | tf_op jit(solution)/shard_map/pallas_call | solution.py:340
  30.5 0.2 collective-permute-start.4
  30.8 0.0 copy-done.8
  30.8 0.1 copy.21.flanks_ref
  30.9 1.3 %collective-permute-done.4.recv_ref = bf16[16,32,256]{2,1,0:T(8,128)(2,1)S(1)} collective-permute-done((bf16[16,32,256]{2,1,0:T(8,128)(2,1)S(1)}, bf16[16,32,256]{2,1,0:T(8,128)(2,1)S(1)}, u32[]{:S(2)}, u32[]{:S(2)}) %collective-permute-start.4) | collective-permute-done | bytes 262176 | tf_op jit(solution)/shard_map/ppermute | solution.py:326
  32.1 0.0 copy-done.2
  32.1 0.0 copy-done.4
  32.1 5.8 %shard_map.115 = (bf16[2,64,256]{2,1,0:T(8,128)(2,1)S(1)}, bf16[2,64,32]{2,1,0:T(8,128)(2,1)S(1)}, bf16[16,64,32]{2,1,0:T(8,128)(2,1)S(1)}) custom-call(s32[1]{0:T(128)} %bitcast.me_ref, bf16[16,32,256]{2,1,0:T(8,128)(2,1)S(1)} %get-tuple-element.7.mine_ref, bf16[16,32,256]{2,1,0:T(8,128)(2,1)S(1)} %collective-permute-done.4.recv_ref, ...), custom_call_target="tpu_custom_call" | custom-call | tf_op jit(solution)/shard_map/pallas_call | solution.py:349
  38.0 0.2 collective-permute-start.5
  38.2 0.2 fusion.2
  38.5 0.2 copy.27
  38.6 0.3 reshape.28
  38.9 0.0 copy-done
  38.9 0.2 fusion.7
  39.1 0.7 %copy.29 = bf16[64,2,256]{2,1,0:T(2,128)(2,1)} copy(bf16[64,2,256]{2,0,1:T(8,128)(2,1)S(1)} %bitcast.44) | data formatting | bytes 131072
  39.8 0.0 collective-permute-done.5
  39.8 0.2 fusion.3
  40.1 0.2 copy.24
  40.2 0.3 reshape.27
  40.5 0.2 broadcast_select_fusion.1
  40.7 0.6 %add_convert_fusion = bf16[2,32,128]{2,1,0:T(8,128)(2,1)} fusion(f32[2,32,128]{2,1,0:T(8,128)S(1)} %bitcast.46, bf16[2,32,128]{2,1,0:T(8,128)(2,1)S(1)} %copy-done.6), kind=kLoop, calls=%fused_computation.20 | loop fusion | flops 24576 | bytes 65536 | tf_op jit(solution)/shard_map/convert_element_type | solution.py:379
  (6 shorter events, 0.1 us)
Async XLA Ops:
  0.6 38.3 %copy-start = (bf16[1024,128]{1,0:T(8,128)(2,1)S(1)}, bf16[1024,128]{1,0:T(8,128)(2,1)}, u32[]{:S(2)}) copy-start(bf16[1024,128]{1,0:T(8,128)(2,1)} %param.19) | copy-start | bytes 786436
  0.6 0.7 %copy-start.9 = (bf16[128,8]{0,1:T(8,128)(2,1)S(1)}, bf16[128,8]{0,1:T(8,128)(2,1)}, u32[]{:S(2)}) copy-start(bf16[128,8]{0,1:T(8,128)(2,1)} %param.13) | copy-start | bytes 6148
  1.4 0.7 %copy-start.6 = (bf16[2,32,128]{2,1,0:T(8,128)(2,1)S(1)}, bf16[2,32,128]{2,1,0:T(8,128)(2,1)}, u32[]{:S(2)}) copy-start(bf16[2,32,128]{2,1,0:T(8,128)(2,1)} %param.11) | copy-start | bytes 49156
  2.1 0.8 %copy-start.5 = (bf16[4,32,256]{2,1,0:T(8,128)(2,1)S(1)}, bf16[4,32,256]{2,1,0:T(8,128)(2,1)}, u32[]{:S(2)}) copy-start(bf16[4,32,256]{2,1,0:T(8,128)(2,1)} %msa_ref.1) | copy-start | bytes 196612
  3.2 8.0 %collective-permute-start = (bf16[1,144,256]{2,1,0:T(8,128)(2,1)S(1)}, bf16[1,144,256]{2,1,0:T(8,128)(2,1)S(1)}, u32[]{:S(2)}, u32[]{:S(2)}) collective-permute-start(bf16[1,144,256]{2,1,0:T(8,128)(2,1)S(1)} %bitcast.40), channel_id=1, source_target_pairs={{0,8},{1,9},{2,10},{3,11},{4,12},{5,13},{6,14},{7,15},{8,0},{9,1},... | collective-permute-start | bytes 221192 | tf_op jit(solution)/shard_map/ppermute | solution.py:326
  11.2 5.2 %collective-permute-start.1 = (bf16[2,144,256]{2,1,0:T(8,128)(2,1)S(1)}, bf16[2,144,256]{2,1,0:T(8,128)(2,1)S(1)}, u32[]{:S(2)}, u32[]{:S(2)}) collective-permute-start(bf16[2,144,256]{2,1,0:T(8,128)(2,1)S(1)} %pad_maximum_fusion.2), channel_id=1, source_target_pairs={{0,4},{1,5},{2,6},{3,7},{4,0},{5,1},{6,2},{7,3},{8,12},{9,13},{10,... | collective-permute-start | bytes 442376 | tf_op jit(solution)/shard_map/ppermute | solution.py:326
  16.5 8.2 %copy-start.1 = (bf16[256,1024]{1,0:T(8,128)(2,1)S(1)}, bf16[256,1024]{1,0:T(8,128)(2,1)}, u32[]{:S(2)}) copy-start(bf16[256,1024]{1,0:T(8,128)(2,1)} %w_ref.2) | copy-start | bytes 1572868
  16.5 8.2 %copy-start.3 = (bf16[256,256]{1,0:T(8,128)(2,1)S(1)}, bf16[256,256]{1,0:T(8,128)(2,1)}, u32[]{:S(2)}) copy-start(bf16[256,256]{1,0:T(8,128)(2,1)} %wo_ref.2) | copy-start | bytes 393220
  16.5 6.8 %collective-permute-start.2 = (bf16[4,144,256]{2,1,0:T(8,128)(2,1)S(1)}, bf16[4,144,256]{2,1,0:T(8,128)(2,1)S(1)}, u32[]{:S(2)}, u32[]{:S(2)}) collective-permute-start(bf16[4,144,256]{2,1,0:T(8,128)(2,1)S(1)} %pad_maximum_fusion.1), channel_id=1, source_target_pairs={{0,2},{1,3},{2,0},{3,1},{4,6},{5,7},{6,4},{7,5},{8,10},{9,11},{10,... | collective-permute-start | bytes 884744 | tf_op jit(solution)/shard_map/ppermute | solution.py:326
  23.3 1.3 %copy-start.7 = (s32[32,256]{1,0:T(8,128)S(1)}, s32[32,256]{1,0:T(8,128)}, u32[]{:S(2)}) copy-start(s32[32,256]{1,0:T(8,128)} %drop_ref.1) | copy-start | bytes 98308
  23.4 7.4 %copy-start.8 = (bf16[256,64]{0,1:T(8,128)(2,1)S(1)}, bf16[256,64]{0,1:T(8,128)(2,1)}, u32[]{:S(2)}) copy-start(bf16[256,64]{0,1:T(8,128)(2,1)} %param.18) | copy-start | bytes 98308
  23.4 8.7 %copy-start.2 = (bf16[256,1024]{1,0:T(8,128)(2,1)S(1)}, bf16[256,1024]{1,0:T(8,128)(2,1)}, u32[]{:S(2)}) copy-start(bf16[256,1024]{1,0:T(8,128)(2,1)} %w_ref.3) | copy-start | bytes 1572868
  23.4 1.2 %collective-permute-start.3 = (bf16[8,8,128]{2,1,0:T(8,128)(2,1)S(1)}, bf16[8,8,128]{2,1,0:T(8,128)(2,1)S(1)}, u32[]{:S(2)}, u32[]{:S(2)}) collective-permute-start(bf16[8,8,128]{2,1,0:T(8,128)(2,1)S(1)} %slice.12), channel_id=1, source_target_pairs={{0,1},{1,0},{2,3},{3,2},{4,5},{5,4},{6,7},{7,6},{8,9},{9,8},{10,11... | collective-permute-start | bytes 49160 | tf_op jit(solution)/shard_map/ppermute | solution.py:326
  24.7 7.5 %copy-start.4 = (bf16[256,256]{1,0:T(8,128)(2,1)S(1)}, bf16[256,256]{1,0:T(8,128)(2,1)}, u32[]{:S(2)}) copy-start(bf16[256,256]{1,0:T(8,128)(2,1)} %wo_ref.3) | copy-start | bytes 393220
  30.5 1.6 %collective-permute-start.4 = (bf16[16,32,256]{2,1,0:T(8,128)(2,1)S(1)}, bf16[16,32,256]{2,1,0:T(8,128)(2,1)S(1)}, u32[]{:S(2)}, u32[]{:S(2)}) collective-permute-start(bf16[16,32,256]{2,1,0:T(8,128)(2,1)S(1)} %get-tuple-element.8), channel_id=1, source_target_pairs={{0,1},{1,0},{2,3},{3,2},{4,5},{5,4},{6,7},{7,6},{8,9},{9,8},{10,11... | collective-permute-start | bytes 786440 | tf_op jit(solution)/shard_map/ppermute | solution.py:326
  38.0 1.8 %collective-permute-start.5 = (bf16[16,64,32]{2,1,0:T(8,128)(2,1)S(1)}, bf16[16,64,32]{2,1,0:T(8,128)(2,1)S(1)}, u32[]{:S(2)}, u32[]{:S(2)}) collective-permute-start(bf16[16,64,32]{2,1,0:T(8,128)(2,1)S(1)} %get-tuple-element.10), channel_id=1, source_target_pairs={{0,1},{1,0},{2,3},{3,2},{4,5},{5,4},{6,7},{7,6},{8,9},{9,8},{10,11... | collective-permute-start | bytes 196616 | tf_op jit(solution)/shard_map/ppermute | solution.py:326

commit v3 on v2

--- a/solution.py
+++ b/solution.py
@@ -182,19 +182,29 @@
     return dot(gated, wo_ref[...])
 
 
-def start_kernel(own, me_ref, msa_ref, pair_ref, wb_ref, out_ref):
+def start_kernel(own, me_ref, msa_hbm, pair_hbm, wb_hbm, out_ref, msa_ref, pair_ref, wb_ref, sems):
+    copies = [
+        pltpu.make_async_copy(pair_hbm, pair_ref, sems.at[0]),
+        pltpu.make_async_copy(wb_hbm, wb_ref, sems.at[1]),
+        pltpu.make_async_copy(msa_hbm, msa_ref, sems.at[2]),
+    ]
+    for copy in copies:
+        copy.start()
     me = me_ref[0]
     seqs, length, features = msa_ref.shape
     order = residue_order(me, length, own)
-    for s in range(seqs):
-        out_ref[s * length : (s + 1) * length, :] = dot(order, msa_ref[s]).astype(BF16)
+    copies[0].wait()
+    copies[1].wait()
     zn = standardise_features(pair_ref[...]).astype(BF16)
-    bias = dot(wb_ref[...], zn, 0, 1)
+    bias = dot(wb_ref[...], zn, 1, 1)
     pad = features - bias.shape[1]
     block = jnp.concatenate([bias, jnp.zeros((bias.shape[0], pad), F32)], axis=1)
     tail = out_ref.shape[0] - seqs * length - bias.shape[0]
     block = jnp.concatenate([block, jnp.zeros((tail, features), F32)], axis=0)
     out_ref[seqs * length :, :] = block.astype(BF16)
+    copies[2].wait()
+    for s in range(seqs):
+        out_ref[s * length : (s + 1) * length, :] = dot(order, msa_ref[s]).astype(BF16)
 
 
 def row_kernel(
@@ -272,7 +282,7 @@
         refresh = gated_attention(x, w_ref, wo_ref, None, total, group)
         aligned = (x + refresh).astype(BF16)
         normed = standardise_features(aligned).astype(BF16)
-        factors = dot(normed, flanks_ref[...]).astype(BF16)
+        factors = dot(normed, flanks_ref[...], 1, 1).astype(BF16)
         for u in range(group):
             al_ref[group * t + u] = aligned[u * total : (u + 1) * total]
             fac_ref[group * t + u] = factors[u * total : (u + 1) * total]
@@ -326,16 +336,30 @@
         return lax.ppermute(x, "dap", [(i, i ^ by) for i in range(devices)])
 
     height = seqs * length + 16
-    buf = pl.pallas_call(
+    hbm = pl.BlockSpec(memory_space=pltpu.HBM)
+    new = pl.pallas_call(
         functools.partial(start_kernel, own),
         out_shape=jax.ShapeDtypeStruct((height, features), BF16),
-        in_specs=[smem, vmem, vmem, vmem],
+        in_specs=[smem, hbm, hbm, hbm],
         out_specs=vmem,
+        scratch_shapes=[
+            pltpu.VMEM((seqs, length, features), BF16),
+            pltpu.VMEM((own * length, channels), BF16),
+            pltpu.VMEM((HEAD_NUMBER, channels), BF16),
+            pltpu.SemaphoreType.DMA((3,)),
+        ],
         compiler_params=params,
-    )(me_arr, homolog_tensor, couple_tensor.reshape(own * length, channels), couple_offset_matrix)
-    buf = buf[None]
-    for by in rounds:
-        buf = jnp.concatenate([buf, swap(buf, by)], axis=0)
+    )(me_arr, homolog_tensor, couple_tensor.reshape(own * length, channels), couple_offset_matrix.T)
+    new = new[None]
+    near = [new]
+    far = []
+    for by in rounds[:-1]:
+        got = swap(jnp.concatenate(near, axis=0), by)
+        far.append(swap(new, rounds[-1]))
+        near.append(got)
+        new = got
+    far.append(swap(new, rounds[-1]))
+    buf = jnp.concatenate(near + far, axis=0)
     other = swap(buf[:, seqs * length : seqs * length + HEAD_NUMBER, :LANES], 1)
     mine, send = pl.pallas_call(
         functools.partial(row_kernel, tuple(rounds), seqs, own),
@@ -360,7 +384,7 @@
             pltpu.VMEM((half, total, 2 * FACTOR_FEATURES), BF16),
         ],
         compiler_params=params,
-    )(me_arr, mine, recv, vertical_attend_matrix, vertical_exit_matrix, averaged_product_flanks)
+    )(me_arr, mine, recv, vertical_attend_matrix, vertical_exit_matrix, averaged_product_flanks.T)
     alignment_output = jnp.swapaxes(align, 0, 1)
     right_other = swap(right, 1)
     right_other = jnp.concatenate([right_other[:, count:], right_other[:, :count]], axis=1)

time: 42.2 us -> 41 us (0.972); the launches traced: 41.4 us -> 40.6 us
  waiting for transfers between devices: 15.8 us -> 11.2 us
  starting transfers between devices: 7.12 us -> 10.2 us
  local copies, waits for them, and re-layouts: 4.08 us -> 4.71 us
    ppermute x6 -> x8, waiting for transfers between devices: 15.8 us -> 11.2 us  [swap(): return lax.ppermute(x, 'dap', [(i, i ^ by) for i in range(devices)])]
    ppermute x6 -> x8, starting transfers between devices: 7.12 us -> 10.2 us  [swap(): return lax.ppermute(x, 'dap', [(i, i ^ by) for i in range(devices)])]
    unnamed x23 -> x28, local copies, waits for them, and re-layouts: 3.14 us -> 3.76 us
  transfers between devices with their start and end apart: 6 -> 8, of which waited for: 5 -> 5; matrix products, arithmetic and copies ran while one was open for 4% -> 4% of each run, Pallas kernels for 0% -> 0%
where the time goes in v3:
time: 41 us; the launch traced here: 40.6 us
  Pallas kernels  12.3 us (30%)
  waiting for transfers between devices  11.2 us (27%)
  starting transfers between devices  10.2 us (25%)
  local copies, waits for them, and re-layouts  4.71 us (11%)
  between operations  0.86 us (2%)
  matrix products  0.81 us (2%)
  other arithmetic  0.65 us (2%)
    ppermute x8, waiting for transfers between devices, swap(): return lax.ppermute(x, 'dap', [(i, i ^ by) for i in range(devices)])  11.2 us
    ppermute x8, starting transfers between devices, swap(): return lax.ppermute(x, 'dap', [(i, i ^ by) for i in range(devices)])  10.2 us
    pallas_call x1, Pallas kernels, small_shards(): pl.pallas_call(functools.partial(row_kernel, tuple(rounds), seqs, own), o...  5.85 us
    pallas_call x1, Pallas kernels, small_shards(): pl.pallas_call(functools.partial(column_kernel, tuple(rounds), seqs, own)...  5.83 us
    unnamed x28, local copies, waits for them, and re-layouts  3.76 us
  transfers between devices with their start and end apart: 8, of which 5 were waited for; matrix products, arithmetic and copies ran while one was open for 4% of the time, Pallas kernels for 0%

profile of v3, /device:TPU:0, one launch (start us, length us, event | category | flops | bytes accessed | tf_op | source)
XLA Modules:
  0.0 40.6 jit_solution(5134403557650389118)
XLA Ops:
  0.6 0.0 copy-start
  0.6 0.0 copy-start.10
  0.7 0.7 %copy-done.10 = bf16[128,8]{0,1:T(8,128)(2,1)S(1)} copy-done((bf16[128,8]{0,1:T(8,128)(2,1)S(1)}, bf16[128,8]{0,1:T(8,128)(2,1)}, u32[]{:S(2)}) %copy-start.10) | copy-done | bytes 2072
  1.4 0.0 copy-start.5
  1.4 0.8 %copy-done.5 = bf16[4,32,256]{2,1,0:T(8,128)(2,1)S(1)} copy-done((bf16[4,32,256]{2,1,0:T(8,128)(2,1)S(1)}, bf16[4,32,256]{2,1,0:T(8,128)(2,1)}, u32[]{:S(2)}) %copy-start.5) | copy-done | bytes 65560
  2.2 0.0 copy-start.6
  2.2 0.7 %copy-done.6 = bf16[2,32,128]{2,1,0:T(8,128)(2,1)S(1)} copy-done((bf16[2,32,128]{2,1,0:T(8,128)(2,1)S(1)}, bf16[2,32,128]{2,1,0:T(8,128)(2,1)}, u32[]{:S(2)}) %copy-start.6) | copy-done | bytes 16408
  2.9 0.6 %shard_map.113 = bf16[144,256]{1,0:T(8,128)(2,1)S(1)} custom-call(s32[1]{0:T(128)} %bitcast.me_ref, bf16[4,32,256]{2,1,0:T(8,128)(2,1)S(1)} %copy-done.5, bf16[64,128]{1,0:T(8,128)(2,1)S(1)} %bitcast.47, bf16[8,128]{1,0:T(8,128)(2,1)S(1)} %bitcast.49), custom_call_target="tpu_custom_call" | custom-call | tf_op jit(solution)/shard_map/pallas_call | solution.py:340
  3.5 4.1 %collective-permute-start = (bf16[1,144,256]{2,1,0:T(8,128)(2,1)S(1)}, bf16[1,144,256]{2,1,0:T(8,128)(2,1)S(1)}, u32[]{:S(2)}, u32[]{:S(2)}) collective-permute-start(bf16[1,144,256]{2,1,0:T(8,128)(2,1)S(1)} %bitcast.43), channel_id=1, source_target_pairs={{0,8},{1,9},{2,10},{3,11},{4,12},{5,13},{6,14},{7,15},{8,0},{9,1},... | collective-permute-start | bytes 221192 | tf_op jit(solution)/shard_map/ppermute | solution.py:336
  7.6 1.5 %collective-permute-start.2 = (bf16[1,144,256]{2,1,0:T(8,128)(2,1)S(1)}, bf16[1,144,256]{2,1,0:T(8,128)(2,1)S(1)}, u32[]{:S(2)}, u32[]{:S(2)}) collective-permute-start(bf16[1,144,256]{2,1,0:T(8,128)(2,1)S(1)} %bitcast.44), channel_id=1, source_target_pairs={{0,2},{1,3},{2,0},{3,1},{4,6},{5,7},{6,4},{7,5},{8,10},{9,11},{10,... | collective-permute-start | bytes 221192 | tf_op jit(solution)/shard_map/ppermute | solution.py:336
  9.2 2.4 %collective-permute-done = bf16[1,144,256]{2,1,0:T(8,128)(2,1)S(1)} collective-permute-done((bf16[1,144,256]{2,1,0:T(8,128)(2,1)S(1)}, bf16[1,144,256]{2,1,0:T(8,128)(2,1)S(1)}, u32[]{:S(2)}, u32[]{:S(2)}) %collective-permute-start) | collective-permute-done | bytes 73760 | tf_op jit(solution)/shard_map/ppermute | solution.py:336
  11.6 0.7 %collective-permute-start.1 = (bf16[2,144,256]{2,1,0:T(8,128)(2,1)S(1)}, bf16[2,144,256]{2,1,0:T(8,128)(2,1)S(1)}, u32[]{:S(2)}, u32[]{:S(2)}) collective-permute-start(bf16[2,144,256]{2,1,0:T(8,128)(2,1)S(1)} %pad_maximum_fusion), channel_id=1, source_target_pairs={{0,4},{1,5},{2,6},{3,7},{4,0},{5,1},{6,2},{7,3},{8,12},{9,13},{10,... | collective-permute-start | bytes 442376 | tf_op jit(solution)/shard_map/ppermute | solution.py:336
  12.3 0.0 copy-start.1
  12.3 1.6 %collective-permute-start.3 = (bf16[1,144,256]{2,1,0:T(8,128)(2,1)S(1)}, bf16[1,144,256]{2,1,0:T(8,128)(2,1)S(1)}, u32[]{:S(2)}, u32[]{:S(2)}) collective-permute-start(bf16[1,144,256]{2,1,0:T(8,128)(2,1)S(1)} %collective-permute-done), channel_id=1, source_target_pairs={{0,2},{1,3},{2,0},{3,1},{4,6},{5,7},{6,4},{7,5},{8,10},{9,11},{10,... | collective-permute-start | bytes 221192 | tf_op jit(solution)/shard_map/ppermute | solution.py:336
  13.9 2.9 %collective-permute-done.1 = bf16[2,144,256]{2,1,0:T(8,128)(2,1)S(1)} collective-permute-done((bf16[2,144,256]{2,1,0:T(8,128)(2,1)S(1)}, bf16[2,144,256]{2,1,0:T(8,128)(2,1)S(1)}, u32[]{:S(2)}, u32[]{:S(2)}) %collective-permute-start.1) | collective-permute-done | bytes 147488 | tf_op jit(solution)/shard_map/ppermute | solution.py:336
  16.8 1.7 %collective-permute-start.4 = (bf16[2,144,256]{2,1,0:T(8,128)(2,1)S(1)}, bf16[2,144,256]{2,1,0:T(8,128)(2,1)S(1)}, u32[]{:S(2)}, u32[]{:S(2)}) collective-permute-start(bf16[2,144,256]{2,1,0:T(8,128)(2,1)S(1)} %collective-permute-done.1), channel_id=1, source_target_pairs={{0,2},{1,3},{2,0},{3,1},{4,6},{5,7},{6,4},{7,5},{8,10},{9,11},{10,... | collective-permute-start | bytes 442376 | tf_op jit(solution)/shard_map/ppermute | solution.py:336
  18.5 0.0 collective-permute-done.2
  18.5 0.0 collective-permute-done.3
  18.6 0.0 copy-start.3
  18.6 3.3 %collective-permute-done.4 = bf16[2,144,256]{2,1,0:T(8,128)(2,1)S(1)} collective-permute-done((bf16[2,144,256]{2,1,0:T(8,128)(2,1)S(1)}, bf16[2,144,256]{2,1,0:T(8,128)(2,1)S(1)}, u32[]{:S(2)}, u32[]{:S(2)}) %collective-permute-start.4) | collective-permute-done | bytes 147488 | tf_op jit(solution)/shard_map/ppermute | solution.py:336
  21.9 0.0 copy-start.8
  22.0 0.0 copy-start.2
  22.0 0.0 copy-start.4
  22.0 0.0 copy-start.9
  22.0 0.1 collective-permute-start.5
  22.1 1.2 %collective-permute-done.5.other_ref = bf16[8,8,128]{2,1,0:T(8,128)(2,1)S(1)} collective-permute-done((bf16[8,8,128]{2,1,0:T(8,128)(2,1)S(1)}, bf16[8,8,128]{2,1,0:T(8,128)(2,1)S(1)}, u32[]{:S(2)}, u32[]{:S(2)}) %collective-permute-start.5) | collective-permute-done | bytes 16416 | tf_op jit(solution)/shard_map/ppermute | solution.py:336
  23.2 0.0 copy-done.1
  23.3 0.0 copy-done.3
  23.3 0.0 copy-done.8
  23.3 5.9 %shard_map.114 = (bf16[16,32,256]{2,1,0:T(8,128)(2,1)S(1)}, bf16[16,32,256]{2,1,0:T(8,128)(2,1)S(1)}) custom-call(s32[1]{0:T(128)} %bitcast.me_ref, bf16[8,144,256]{2,1,0:T(8,128)(2,1)S(1)} %constant_dynamic-update-slice_fusion.buf_ref, bf16[8,8,128]{2,1,0:T(8,128)(2,1)S(1)} %collective-permute-done.5.other_ref, bf16[256,1024]{1,0:T(8,128)(2,1)S(1)} %copy-done.1, ...), custom_call_target="tpu_custom_call" | custom-call | tf_op jit(solution)/shard_map/pallas_call | solution.py:364
  29.1 0.2 collective-permute-start.6
  29.3 1.4 %collective-permute-done.6.recv_ref = bf16[16,32,256]{2,1,0:T(8,128)(2,1)S(1)} collective-permute-done((bf16[16,32,256]{2,1,0:T(8,128)(2,1)S(1)}, bf16[16,32,256]{2,1,0:T(8,128)(2,1)S(1)}, u32[]{:S(2)}, u32[]{:S(2)}) %collective-permute-start.6) | collective-permute-done | bytes 262176 | tf_op jit(solution)/shard_map/ppermute | solution.py:336
  30.7 0.0 copy-done.2
  30.7 0.0 copy-done.4
  30.7 0.0 copy-done.9
  30.7 5.8 %shard_map.115 = (bf16[2,64,256]{2,1,0:T(8,128)(2,1)S(1)}, bf16[2,64,32]{2,1,0:T(8,128)(2,1)S(1)}, bf16[16,64,32]{2,1,0:T(8,128)(2,1)S(1)}) custom-call(s32[1]{0:T(128)} %bitcast.me_ref, bf16[16,32,256]{2,1,0:T(8,128)(2,1)S(1)} %get-tuple-element.7.mine_ref, bf16[16,32,256]{2,1,0:T(8,128)(2,1)S(1)} %collective-permute-done.6.recv_ref, ...), custom_call_target="tpu_custom_call" | custom-call | tf_op jit(solution)/shard_map/pallas_call | solution.py:373
  36.6 0.2 collective-permute-start.7
  36.8 0.3 fusion.2
  37.1 0.2 copy.23
  37.2 0.3 reshape.28
  37.5 0.0 copy-done
  37.5 0.2 fusion.7
  37.7 0.7 %copy.25 = bf16[64,2,256]{2,1,0:T(2,128)(2,1)} copy(bf16[64,2,256]{2,0,1:T(8,128)(2,1)S(1)} %bitcast.46) | data formatting | bytes 131072
  38.4 0.0 collective-permute-done.7
  38.4 0.3 fusion.3
  38.7 0.2 copy.20
  38.8 0.3 reshape.27
  39.1 0.2 broadcast_select_fusion.1
  39.3 0.0 copy-start.7
  39.4 0.7 %copy-done.7 = bf16[2,32,128]{2,1,0:T(8,128)(2,1)S(1)} copy-done((bf16[2,32,128]{2,1,0:T(8,128)(2,1)S(1)}, bf16[2,32,128]{2,1,0:T(8,128)(2,1)}, u32[]{:S(2)}) %copy-start.7) | copy-done | bytes 16408
  40.0 0.6 %add_convert_fusion = bf16[2,32,128]{2,1,0:T(8,128)(2,1)} fusion(f32[2,32,128]{2,1,0:T(8,128)S(1)} %bitcast.50, bf16[2,32,128]{2,1,0:T(8,128)(2,1)S(1)} %copy-done.7), kind=kLoop, calls=%fused_computation.18 | loop fusion | flops 24576 | bytes 65536 | tf_op jit(solution)/shard_map/convert_element_type | solution.py:403
  (11 shorter events, 0.1 us)
Async XLA Ops:
  0.6 36.9 %copy-start = (bf16[1024,128]{1,0:T(8,128)(2,1)S(1)}, bf16[1024,128]{1,0:T(8,128)(2,1)}, u32[]{:S(2)}) copy-start(bf16[1024,128]{1,0:T(8,128)(2,1)} %param.19) | copy-start | bytes 786436
  0.6 0.7 %copy-start.10 = (bf16[128,8]{0,1:T(8,128)(2,1)S(1)}, bf16[128,8]{0,1:T(8,128)(2,1)}, u32[]{:S(2)}) copy-start(bf16[128,8]{0,1:T(8,128)(2,1)} %param.13) | copy-start | bytes 6148
  1.4 0.8 %copy-start.5 = (bf16[4,32,256]{2,1,0:T(8,128)(2,1)S(1)}, bf16[4,32,256]{2,1,0:T(8,128)(2,1)}, u32[]{:S(2)}) copy-start(bf16[4,32,256]{2,1,0:T(8,128)(2,1)} %msa_hbm.1) | copy-start | bytes 196612
  2.2 0.7 %copy-start.6 = (bf16[2,32,128]{2,1,0:T(8,128)(2,1)S(1)}, bf16[2,32,128]{2,1,0:T(8,128)(2,1)}, u32[]{:S(2)}) copy-start(bf16[2,32,128]{2,1,0:T(8,128)(2,1)} %param.11) | copy-start | bytes 49156
  3.5 8.0 %collective-permute-start = (bf16[1,144,256]{2,1,0:T(8,128)(2,1)S(1)}, bf16[1,144,256]{2,1,0:T(8,128)(2,1)S(1)}, u32[]{:S(2)}, u32[]{:S(2)}) collective-permute-start(bf16[1,144,256]{2,1,0:T(8,128)(2,1)S(1)} %bitcast.43), channel_id=1, source_target_pairs={{0,8},{1,9},{2,10},{3,11},{4,12},{5,13},{6,14},{7,15},{8,0},{9,1},... | collective-permute-start | bytes 221192 | tf_op jit(solution)/shard_map/ppermute | solution.py:336
  7.6 10.9 %collective-permute-start.2 = (bf16[1,144,256]{2,1,0:T(8,128)(2,1)S(1)}, bf16[1,144,256]{2,1,0:T(8,128)(2,1)S(1)}, u32[]{:S(2)}, u32[]{:S(2)}) collective-permute-start(bf16[1,144,256]{2,1,0:T(8,128)(2,1)S(1)} %bitcast.44), channel_id=1, source_target_pairs={{0,2},{1,3},{2,0},{3,1},{4,6},{5,7},{6,4},{7,5},{8,10},{9,11},{10,... | collective-permute-start | bytes 221192 | tf_op jit(solution)/shard_map/ppermute | solution.py:336
  11.6 5.2 %collective-permute-start.1 = (bf16[2,144,256]{2,1,0:T(8,128)(2,1)S(1)}, bf16[2,144,256]{2,1,0:T(8,128)(2,1)S(1)}, u32[]{:S(2)}, u32[]{:S(2)}) collective-permute-start(bf16[2,144,256]{2,1,0:T(8,128)(2,1)S(1)} %pad_maximum_fusion), channel_id=1, source_target_pairs={{0,4},{1,5},{2,6},{3,7},{4,0},{5,1},{6,2},{7,3},{8,12},{9,13},{10,... | collective-permute-start | bytes 442376 | tf_op jit(solution)/shard_map/ppermute | solution.py:336
  12.3 11.0 %copy-start.1 = (bf16[256,1024]{1,0:T(8,128)(2,1)S(1)}, bf16[256,1024]{1,0:T(8,128)(2,1)}, u32[]{:S(2)}) copy-start(bf16[256,1024]{1,0:T(8,128)(2,1)} %w_ref.2) | copy-start | bytes 1572868
  12.3 6.2 %collective-permute-start.3 = (bf16[1,144,256]{2,1,0:T(8,128)(2,1)S(1)}, bf16[1,144,256]{2,1,0:T(8,128)(2,1)S(1)}, u32[]{:S(2)}, u32[]{:S(2)}) collective-permute-start(bf16[1,144,256]{2,1,0:T(8,128)(2,1)S(1)} %collective-permute-done), channel_id=1, source_target_pairs={{0,2},{1,3},{2,0},{3,1},{4,6},{5,7},{6,4},{7,5},{8,10},{9,11},{10,... | collective-permute-start | bytes 221192 | tf_op jit(solution)/shard_map/ppermute | solution.py:336
  16.8 5.1 %collective-permute-start.4 = (bf16[2,144,256]{2,1,0:T(8,128)(2,1)S(1)}, bf16[2,144,256]{2,1,0:T(8,128)(2,1)S(1)}, u32[]{:S(2)}, u32[]{:S(2)}) collective-permute-start(bf16[2,144,256]{2,1,0:T(8,128)(2,1)S(1)} %collective-permute-done.1), channel_id=1, source_target_pairs={{0,2},{1,3},{2,0},{3,1},{4,6},{5,7},{6,4},{7,5},{8,10},{9,11},{10,... | collective-permute-start | bytes 442376 | tf_op jit(solution)/shard_map/ppermute | solution.py:336
  18.6 4.7 %copy-start.3 = (bf16[256,256]{1,0:T(8,128)(2,1)S(1)}, bf16[256,256]{1,0:T(8,128)(2,1)}, u32[]{:S(2)}) copy-start(bf16[256,256]{1,0:T(8,128)(2,1)} %wo_ref.2) | copy-start | bytes 393220
  21.9 1.3 %copy-start.8 = (s32[32,256]{1,0:T(8,128)S(1)}, s32[32,256]{1,0:T(8,128)}, u32[]{:S(2)}) copy-start(s32[32,256]{1,0:T(8,128)} %drop_ref.1) | copy-start | bytes 98308
  22.0 8.8 %copy-start.2 = (bf16[256,1024]{1,0:T(8,128)(2,1)S(1)}, bf16[256,1024]{1,0:T(8,128)(2,1)}, u32[]{:S(2)}) copy-start(bf16[256,1024]{1,0:T(8,128)(2,1)} %w_ref.3) | copy-start | bytes 1572868
  22.0 8.8 %copy-start.4 = (bf16[256,256]{1,0:T(8,128)(2,1)S(1)}, bf16[256,256]{1,0:T(8,128)(2,1)}, u32[]{:S(2)}) copy-start(bf16[256,256]{1,0:T(8,128)(2,1)} %wo_ref.3) | copy-start | bytes 393220
  22.0 8.7 %copy-start.9 = (bf16[256,64]{0,1:T(8,128)(2,1)S(1)}, bf16[256,64]{0,1:T(8,128)(2,1)}, u32[]{:S(2)}) copy-start(bf16[256,64]{0,1:T(8,128)(2,1)} %param.18) | copy-start | bytes 98308
  22.0 1.2 %collective-permute-start.5 = (bf16[8,8,128]{2,1,0:T(8,128)(2,1)S(1)}, bf16[8,8,128]{2,1,0:T(8,128)(2,1)S(1)}, u32[]{:S(2)}, u32[]{:S(2)}) collective-permute-start(bf16[8,8,128]{2,1,0:T(8,128)(2,1)S(1)} %slice.12), channel_id=1, source_target_pairs={{0,1},{1,0},{2,3},{3,2},{4,5},{5,4},{6,7},{7,6},{8,9},{9,8},{10,11... | collective-permute-start | bytes 49160 | tf_op jit(solution)/shard_map/ppermute | solution.py:336
  29.1 1.6 %collective-permute-start.6 = (bf16[16,32,256]{2,1,0:T(8,128)(2,1)S(1)}, bf16[16,32,256]{2,1,0:T(8,128)(2,1)S(1)}, u32[]{:S(2)}, u32[]{:S(2)}) collective-permute-start(bf16[16,32,256]{2,1,0:T(8,128)(2,1)S(1)} %get-tuple-element.8), channel_id=1, source_target_pairs={{0,1},{1,0},{2,3},{3,2},{4,5},{5,4},{6,7},{7,6},{8,9},{9,8},{10,11... | collective-permute-start | bytes 786440 | tf_op jit(solution)/shard_map/ppermute | solution.py:336
  36.6 1.8 %collective-permute-start.7 = (bf16[16,64,32]{2,1,0:T(8,128)(2,1)S(1)}, bf16[16,64,32]{2,1,0:T(8,128)(2,1)S(1)}, u32[]{:S(2)}, u32[]{:S(2)}) collective-permute-start(bf16[16,64,32]{2,1,0:T(8,128)(2,1)S(1)} %get-tuple-element.10), channel_id=1, source_target_pairs={{0,1},{1,0},{2,3},{3,2},{4,5},{5,4},{6,7},{7,6},{8,9},{9,8},{10,11... | collective-permute-start | bytes 196616 | tf_op jit(solution)/shard_map/ppermute | solution.py:336
  39.3 0.7 %copy-start.7 = (bf16[2,32,128]{2,1,0:T(8,128)(2,1)S(1)}, bf16[2,32,128]{2,1,0:T(8,128)(2,1)}, u32[]{:S(2)}) copy-start(bf16[2,32,128]{2,1,0:T(8,128)(2,1)} %param.11) | copy-start | bytes 49156
